TPU v7x, 256 devices: a whole 4x4x8 slice. The times are simulated.
256 devices in a mesh: seq: 8 (over y, core), space: 32 (over z, x).
Axes of the slice: x: 4, y: 4, z: 8, core: 2. Of those that a mesh axis runs over, the one named last changes fastest.
Arguments:
- features: bfloat16 [2048, 65536], P(None, ('seq', 'space')), may hold values from -6 to 6
- targets: bfloat16 [2048, 65536], P(None, ('seq', 'space')), may hold values from -6 to 6
- write_keys: bfloat16 [128, 65536], P(None, ('seq', 'space')), may hold values from -0.5 to 0.5
- read_queries: bfloat16 [128, 65536], P(None, ('seq', 'space')), may hold values from -0.0234375 to 0.0234375
- decay_codes: int32 [32, 65536], P('space', 'seq'), may hold values from 0 to 99, as said below
- scan_order: int32 [8192], replicated, may hold values from 0 to 8191, each once
- masked: int32 [49152], P(('seq', 'space')), may hold values from 0 to 65535, as said below
- skip_gain: float32 [32], P('space'), may hold values from 0.5 to 1.5
Outputs:
- mixed: bfloat16 [2048, 65536], P(None, ('seq', 'space'))
- grad_features: bfloat16 [2048, 65536], P(None, ('seq', 'space'))
Inputs may be any that keep to these rules, and one draw needn't show every extreme that they name: `decay_codes`: a token's decay factor for its head is exp(-(0.065536 / 65536) code). `masked`: entries k * 192 to (k + 1) * 192 - 1 are distinct indices among tokens k * 256 to (k + 1) * 256 - 1.
All inputs are finite; a program needn't handle non-finite values.
Results may differ from a plain program's by a relative error of at most 0.0034.
Values may be sent and summed in bfloat16 or wider, within the bound.
No kernel may reach another device: no remote copies, remote signals or barrier semaphores. Data moves between devices by JAX's collectives and lax.ppermute only.
A program may use at most 128 MiB of HBM per device.

v0:
```python
from functools import partial

import jax
import jax.numpy as jnp
from jax import lax
from jax.experimental import pallas as pl
from jax.experimental.pallas import tpu as pltpu
from jax.sharding import PartitionSpec as P

BLOCK = 512
MARK = 16384.0
f32, bf16 = jnp.float32, jnp.bfloat16
anywhere = pl.BlockSpec(memory_space=pl.ANY)
smem = pl.BlockSpec(memory_space=pltpu.SMEM)


def call(kernel, outs, scalars, arrays, scratch, flops, name):
    args = [*scalars, *arrays]
    moved = sum(a.size * a.dtype.itemsize for a in args)
    moved += sum(o.size * o.dtype.itemsize for o in outs)
    held = [pltpu.VMEM(v.shape, v.dtype) for v in [*arrays, *outs]]
    most = max(v.shape[0] for v in [*arrays, *outs])
    sems = pltpu.SemaphoreType.DMA((len(held), most))
    return pl.pallas_call(
        partial(streaming, kernel, len(scalars), len(arrays), len(outs)),
        out_shape=outs,
        in_specs=[smem] * len(scalars) + [anywhere] * len(arrays),
        out_specs=[anywhere] * len(outs),
        scratch_shapes=[*held, sems, *scratch],
        cost_estimate=pl.CostEstimate(flops=flops, bytes_accessed=moved, transcendentals=0),
        name=name,
    )(*args)


class Stream:
    def __init__(self, far, near, sems):
        self.far, self.near, self.sems = far, near, sems
        self.count, self.shape = near.shape[0], near.shape

    def each(self, act):
        lax.fori_loop(0, self.count, lambda i, _: (act(i), 0)[1], 0)

    def inward(self, i):
        return pltpu.make_async_copy(self.far.at[i], self.near.at[i], self.sems.at[i])

    def outward(self, i):
        return pltpu.make_async_copy(self.near.at[i], self.far.at[i], self.sems.at[i])

    def __getitem__(self, i):
        return self.near[i]

    def take(self, i):
        self.inward(i).wait()
        return self.near[i]

    def give(self, i, value):
        self.near[i] = value
        self.outward(i).start()


def streaming(kernel, n_scalars, n_in, n_out, *refs):
    scalars, refs = refs[:n_scalars], refs[n_scalars:]
    far, refs = refs[: n_in + n_out], refs[n_in + n_out :]
    near, sems, scratch = refs[: n_in + n_out], refs[n_in + n_out], refs[n_in + n_out + 1 :]
    streams = [Stream(f, n, sems.at[k]) for k, (f, n) in enumerate(zip(far, near))]
    for stream in streams[:n_in]:
        stream.each(lambda i, s=stream: s.inward(i).start())
    kernel(*scalars, *streams, *scratch)
    for stream in streams[n_in:]:
        stream.each(lambda i, s=stream: s.outward(i).wait())


def struct(shape, dtype):
    return jax.ShapeDtypeStruct(shape, dtype)


def left_half(shape):
    return lax.broadcasted_iota(jnp.int32, shape, 1) < shape[1] // 2


def lower_part(shape):
    return lax.broadcasted_iota(jnp.int32, shape, 0) >= lax.broadcasted_iota(jnp.int32, shape, 1)


def split(value):
    high = value.astype(bf16)
    return high, (value - high.astype(f32)).astype(bf16)


def gather_rows(order, b, src, dst):
    first = b * BLOCK
    for i in range(BLOCK):
        dst[i // 8, pl.ds(i % 8, 1), :] = src[pl.ds(order[first + i], 1), :]


def scatter_rows(order, b, src, dst):
    first = b * BLOCK
    for i in range(BLOCK):
        dst[pl.ds(order[first + i], 1), :] = src[i // 8, pl.ds(i % 8, 1), :]


def gathered_blocks(order, count, src, bufs, work, init):
    gather_rows(order, 0, src, bufs[0])

    def pair(i, carry):
        for k in range(2):
            b = 2 * i + k
            block = bufs[k][...].reshape(BLOCK, 128)
            gather_rows(order, jnp.minimum(b + 1, count - 1), src, bufs[1 - k])
            carry = work(b, block, carry)
        return carry

    return lax.fori_loop(0, count // 2, pair, init)


def scattered_blocks(order, count, bufs, dst, work):
    def put(k, value):
        bufs[k][...] = value.reshape(BLOCK // 8, 8, 128)

    put(0, work(0))
    put(1, work(1))
    scatter_rows(order, 0, bufs[0], dst)

    def pair(i, _):
        for k in range(2):
            b = 2 * i + k
            scatter_rows(order, b - 1, bufs[1 - k], dst)
            put(k, work(b))
        return 0

    lax.fori_loop(1, count // 2, pair, 0)
    scatter_rows(order, count - 1, bufs[1], dst)


def packet_kernel(write, read, out):
    for k, side in enumerate((write, read)):
        out.give(k, side.take(0).astype(f32).T.astype(bf16))


def decay_kernel(unit, order, codes, e_out, total_out, code_all, tri, *bufs):
    def load(c, sums):
        row = codes.take(c)
        code_all[pl.ds(pl.multiple_of(c * 128, 128), 128), :] = jnp.broadcast_to(row, (128, 128)).T
        return sums + row

    sums = lax.fori_loop(0, codes.count, load, jnp.zeros((1, 128), f32))
    tri[...] = jnp.where(lower_part((BLOCK, BLOCK)), 1.0, 0.0).astype(bf16)
    total = jnp.sum(sums)
    total_out.give(0, jnp.full((8, 128), total, f32))
    rate = jnp.where(left_half((BLOCK, 128)), unit, -unit)

    def block(b, code, earlier):
        reach = jnp.dot(tri[...], code.astype(bf16), preferred_element_type=f32) + earlier
        e_out.give(b, jnp.exp(rate * (reach - 0.5 * total)))
        return reach[BLOCK - 1 : BLOCK, :]

    gathered_blocks(order, e_out.count, code_all, bufs, block, jnp.zeros((1, 128), f32))


def rows_kernel(order, values, targets, xt_out, xt_all, *bufs):
    tok = values.shape[2]

    def load(c, _):
        base = pl.multiple_of(c * tok, tok)
        both = jnp.concatenate([values.take(c).astype(f32), targets.take(c).astype(f32)], axis=0)
        xt_all[pl.ds(base, tok), :] = both.T
        return 0

    lax.fori_loop(0, values.count, load, 0)

    def block(b, rows, _):
        xt_out.give(b, rows.astype(bf16))
        return 0

    gathered_blocks(order, xt_out.count, xt_all, bufs, block, 0)


def block_states(scaled, into_t):
    p = jnp.dot(into_t, jnp.concatenate(split(scaled), axis=1), preferred_element_type=f32)
    return p[:, :128] + p[:, 128:]


def lower_sum(scaled, from_side, into_t):
    gram = jnp.dot(from_side, into_t, preferred_element_type=f32)
    gram = jnp.where(lower_part((BLOCK, BLOCK)), gram, 0.0).astype(bf16)
    return jnp.dot(gram, scaled.astype(bf16), preferred_element_type=f32)


def unpack(sides, side, rows_all):
    tok = sides.shape[2]

    def load(c, _):
        rows_all[pl.ds(pl.multiple_of(c * tok, tok), tok), :] = sides.take(c)[side].astype(f32)
        return 0

    lax.fori_loop(0, sides.count, load, 0)


def doubled(xt):
    x = xt.astype(f32)
    return jnp.where(left_half((BLOCK, 128)), x, pltpu.roll(x, 64, 1))


def states_kernel(order, write, xt_in, e_in, total, w_out, wt_out, p_out, pay_out, rows_all, *bufs):
    unpack(write, 0, rows_all)

    def block(b, w, summed):
        w_t = w.T.astype(bf16)
        w_out.give(b, w.astype(bf16))
        wt_out.give(b, w_t)
        p = block_states(doubled(xt_in.take(b)) * e_in.take(b), w_t)
        p_out.give(b, p)
        return summed + p

    summed = gathered_blocks(order, p_out.count, rows_all, bufs, block, jnp.zeros((128, 128), f32))
    pay_out.give(0, jnp.concatenate([summed, total.take(0)], axis=0))


def near_kernel(order, read, xt_in, e_in, wt_in, q_out, qt_out, near_out, rows_all, *bufs):
    unpack(read, 1, rows_all)

    def block(b, q, _):
        q_low = q.astype(bf16)
        q_out.give(b, q_low)
        qt_out.give(b, q.T.astype(bf16))
        scaled = doubled(xt_in.take(b)) * e_in.take(b)
        near_out.give(b, lower_sum(scaled, q_low, wt_in.take(b)))
        return 0

    gathered_blocks(order, near_out.count, rows_all, bufs, block, 0)


def prepare(unit, me, p_in, others_in, fr):
    groups, blocks = others_in.count, p_in.count
    others = [others_in.take(g) for g in range(groups)]
    half = left_half((1, 128))
    centers = []
    before = jnp.zeros((1, 128), f32)
    for g in range(groups):
        size = others[g][128:129, :]
        centers.append(before + 0.5 * size)
        before = before + size
    mine = jnp.zeros((1, 128), f32)
    for g in range(groups):
        mine = mine + jnp.where(me == g, centers[g], 0.0)
    init = jnp.zeros((128, 128), f32)
    for g in range(groups):
        factor = jnp.exp(-unit * jnp.abs(mine - centers[g]))
        ahead = jnp.where(g < me, factor, 0.0)
        behind = jnp.where(g > me, factor, 0.0)
        init = init + others[g][0:128, :] * jnp.where(half, ahead, behind)
    left = left_half((128, 128))

    def forward(b, run):
        fr[b, :, 0:128] = run
        return run + p_in.take(b)

    lax.fori_loop(0, blocks, forward, init)

    def backward(i, run):
        b = blocks - 1 - i
        run = run + p_in[b]
        high, low = split(jnp.where(left, fr[b, :, 0:128], run))
        fr[b, :, 0:128] = high.astype(f32)
        fr[b, :, 128:256] = low.astype(f32)
        return run

    lax.fori_loop(0, blocks, backward, init)


def read_out(from_side, fr, near, e):
    read = jnp.dot(from_side, fr.astype(bf16), preferred_element_type=f32)
    z = read[:, :128] + read[:, 128:]
    z = z + jnp.where(left_half((BLOCK, 128)), near, -near)
    z = z * pltpu.roll(e, 64, 1)
    return z + pltpu.roll(z, 64, 1)


def store_positions(y_all, out):
    tok = out.shape[2]

    def store(c, _):
        base = pl.multiple_of(c * tok, tok)
        out.give(c, y_all[pl.ds(base, tok), :].T[0:64, :].astype(bf16))
        return 0

    lax.fori_loop(0, out.count, store, 0)


def turn_kernel(unit, where, skip, from_in, from_t, xt_in, e_in, near_in, p_in, total, others, y_out, res_out, p_out, pay_out, fr):
    prepare(unit, where[0], p_in, others, fr)
    gain = skip[0]
    left = left_half((BLOCK, 128))

    def block(b, summed):
        e = e_in.take(b)
        xt = xt_in.take(b).astype(f32)
        tx = pltpu.roll(xt, 64, 1)
        x = jnp.where(left, xt, tx)
        t = jnp.where(left, tx, xt)
        y = (read_out(from_in.take(b), fr[b], near_in.take(b), e) + gain * x).astype(bf16)
        y_out.give(b, y)
        residue = jnp.where(t < 1024.0, y.astype(f32) - t, 0.0).astype(bf16)
        res_out.give(b, residue)
        p = block_states(residue.astype(f32) * e, from_t.take(b))
        p_out.give(b, p)
        return summed + p

    summed = lax.fori_loop(0, p_in.count, block, jnp.zeros((128, 128), f32))
    pay_out.give(0, jnp.concatenate([summed, total.take(0)], axis=0))


def place_kernel(order, y_in, res_in, e_in, into_in, from_t, out, near_out, y_all, *bufs):
    def block(b):
        scaled = res_in.take(b).astype(f32) * e_in.take(b)
        near_out.give(b, lower_sum(scaled, into_in.take(b), from_t.take(b)))
        return y_in.take(b).astype(f32)

    scattered_blocks(order, near_out.count, bufs, y_all, block)
    store_positions(y_all, out)


def finish_kernel(unit, order, where, skip, into_in, res_in, e_in, near_in, p_in, others, out, fr, y_all, *bufs):
    prepare(unit, where[0], p_in, others, fr)
    gain = skip[0]

    def block(b):
        y = read_out(into_in.take(b), fr[b], near_in.take(b), e_in.take(b))
        return y + gain * res_in.take(b).astype(f32)

    scattered_blocks(order, p_in.count, bufs, y_all, block)
    store_positions(y_all, out)


def per_device(
    features, targets, write_keys, read_queries, decay_codes, scan_order, masked, skip_gain
):
    space_size = lax.axis_size("space")
    seq_size = lax.axis_size("seq")
    state = write_keys.shape[0]
    tok = features.shape[1]
    length = tok * space_size
    blocks = length // BLOCK
    unit = 0.065536 / (length * seq_size)
    width = features.shape[0] // space_size
    seq_place = lax.axis_index("seq")
    first_token = (seq_place * space_size + lax.axis_index("space")) * tok

    def swap(a, axis):
        return lax.all_to_all(a, axis, split_axis=0, concat_axis=0, tiled=True)

    packet = call(
        packet_kernel, [struct((2, tok, state), bf16)], [], [write_keys[None], read_queries[None]], [], 0, "packet"
    )[0]
    gathered = lax.all_gather(packet, "space", axis=0, tiled=False)
    head_x = swap(features.reshape(space_size, width, tok), "space")
    slot_grid = lax.broadcasted_iota(jnp.int32, (masked.shape[0], tok), 1)
    is_masked = jnp.any((masked - first_token)[:, None] == slot_grid, axis=0)
    marked = jnp.where(is_masked[None], targets, jnp.asarray(MARK, bf16))
    head_t = swap(marked.reshape(space_size, width, tok), "space")
    codes = decay_codes.astype(f32).reshape(length // 128, 1, 128)
    where = seq_place.reshape(1).astype(jnp.int32)

    by_block = struct((blocks, BLOCK, state), bf16)
    wide = struct((blocks, BLOCK, 128), f32)
    by_block_t = struct((blocks, state, BLOCK), bf16)
    states = struct((blocks, state, 128), f32)
    payload = struct((1, state + 8, 128), f32)
    heads = struct((space_size, width, tok), bf16)
    small = pltpu.VMEM((BLOCK // 8, 8, 128), f32)
    full = pltpu.VMEM((length, 128), f32)
    read_states = pltpu.VMEM((blocks, state, 256), f32)

    e, total = call(
        partial(decay_kernel, unit),
        [wide, struct((1, 8, 128), f32)],
        [scan_order],
        [codes],
        [full, pltpu.VMEM((BLOCK, BLOCK), bf16), small, small],
        2 * 10**9,
        "decay",
    )
    xt = call(rows_kernel, [by_block], [scan_order], [head_x, head_t], [full, small, small], 10**9, "rows")[0]
    w, w_t, p, pay = call(
        states_kernel,
        [by_block, by_block_t, states, payload],
        [scan_order],
        [gathered, xt, e, total],
        [full, small, small],
        2 * 10**9,
        "states",
    )
    others = swap(jnp.broadcast_to(pay, (seq_size,) + pay.shape[1:]), "seq")
    q, q_t, near = call(
        near_kernel,
        [by_block, by_block_t, wide],
        [scan_order],
        [gathered, xt, e, w_t],
        [full, small, small],
        4 * 10**9,
        "near",
    )
    y, residue, p, pay = call(
        partial(turn_kernel, unit),
        [by_block, by_block, states, payload],
        [where, skip_gain],
        [q, q_t, xt, e, near, p, total, others],
        [read_states],
        2 * 10**9,
        "turn",
    )
    others = swap(jnp.broadcast_to(pay, (seq_size,) + pay.shape[1:]), "seq")
    mixed_heads, near = call(
        place_kernel,
        [heads, wide],
        [scan_order],
        [y, residue, e, w, q_t],
        [full, small, small],
        4 * 10**9,
        "place",
    )
    mixed = swap(mixed_heads, "space").reshape(features.shape)
    grads_heads = call(
        partial(finish_kernel, unit),
        [heads],
        [scan_order, where, skip_gain],
        [w, residue, e, near, p, others],
        [read_states, full, small, small],
        2 * 10**9,
        "finish",
    )[0]
    grad_features = swap(grads_heads, "space").reshape(features.shape)
    return (mixed, grad_features)


def solution(mesh):
    return jax.shard_map(
        per_device,
        mesh=mesh,
        in_specs=(
            P(None, ("seq", "space")),
            P(None, ("seq", "space")),
            P(None, ("seq", "space")),
            P(None, ("seq", "space")),
            P("space", "seq"),
            P(),
            P(("seq", "space")),
            P("space"),
        ),
        out_specs=(P(None, ("seq", "space")), P(None, ("seq", "space"))),
        check_vma=False,
    )
```

profile of v0, /device:TPU:2, one launch (start us, length us, event | category | flops | bytes accessed | tf_op | source)
XLA Modules:
  0.0 286.8 jit_solution(6036643731871531980)
XLA Ops:
  7.2 1.7 packet.1
  9.8 1.3 broadcast_select_fusion
  11.1 44.0 %all_to_all.30.refs_2_ = bf16[32,64,256]{2,1,0:T(8,128)(2,1)} all-to-all(bf16[32,64,256]{2,1,0:T(8,128)(2,1)S(1)} %bitcast.14), channel_id=1, replica_groups=mesh['seq'=8,'space'=32] {'space'}, dimensions={0} | all-to-all | bytes 2097152 | tf_op jit(solution)/shard_map/all_to_all | solution.py:350
  55.1 5.6 %all-to-all-start = ((bf16[32,64,256]{2,1,0:T(8,128)(2,1)}), bf16[32,64,256]{2,1,0:T(8,128)(2,1)S(1)}, u32[]{:S(2)}, u32[]{:S(2)}) async-start(bf16[32,64,256]{2,1,0:T(8,128)(2,1)} %bitcast.4), calls=%async_computation | async-start | bytes 2097152 | tf_op jit(solution)/shard_map/all_to_all | solution.py:350
  61.3 21.1 %decay.1 = (f32[16,512,128]{2,1,0:T(8,128)}, f32[1,8,128]{2,1,0:T(8,128)}) custom-call(s32[8192]{0:T(1024)} %refs_0_.11, f32[64,1,128]{2,1,0:T(1,128)} %convert_bitcast_fusion.refs_1_), custom_call_target="tpu_custom_call" | custom-call | flops 2000000000 | bytes 4263936 | tf_op jit(solution)/shard_map/decay/pallas_call | solution.py:24
  82.4 13.4 %all-to-all-done.refs_1_ = bf16[32,64,256]{2,1,0:T(8,128)(2,1)S(1)} async-done(((bf16[32,64,256]{2,1,0:T(8,128)(2,1)}), bf16[32,64,256]{2,1,0:T(8,128)(2,1)S(1)}, u32[]{:S(2)}, u32[]{:S(2)}) %all-to-all-start) | async-done | bytes 1048608 | tf_op jit(solution)/shard_map/all_to_all | solution.py:350
  95.7 1.0 copy-done
  96.7 14.1 %rows.1.refs_2_.refs_4_ = bf16[16,512,128]{2,1,0:T(8,128)(2,1)} custom-call(s32[8192]{0:T(1024)} %refs_0_.11, bf16[32,64,256]{2,1,0:T(8,128)(2,1)} %copy-done, bf16[32,64,256]{2,1,0:T(8,128)(2,1)} %all_to_all.30.refs_2_), custom_call_target="tpu_custom_call" | custom-call | flops 1000000000 | bytes 4227072 | tf_op jit(solution)/shard_map/rows/pallas_call | solution.py:24
  110.9 17.1 %states.1 = (bf16[16,512,128]{2,1,0:T(8,128)(2,1)}, bf16[16,128,512]{2,1,0:T(8,128)(2,1)}, f32[16,128,128]{2,1,0:T(8,128)}, f32[1,136,128]{2,1,0:T(8,128)}) custom-call(s32[8192]{0:T(1024)} %refs_0_.11, bf16[32,2,256,128]{3,2,1,0:T(8,128)(2,1)} %bitcast.12, bf16[16,512,128]{2,1,0:T(8,128)(2,1)} %rows.1.refs_2_.refs_4_, ...), custom_call_target="tpu_custom_call" | custom-call | flops 2000000000 | bytes 15835136 | tf_op jit(solution)/shard_map/states/pallas_call | solution.py:24
  127.9 1.7 broadcast_in_dim.39
  129.7 4.6 %all-to-all-start.2 = ((f32[8,136,128]{2,1,0:T(8,128)}), f32[8,136,128]{2,1,0:T(8,128)S(1)}, u32[]{:S(2)}, u32[]{:S(2)}) async-start(f32[8,136,128]{2,1,0:T(8,128)} %broadcast_in_dim.39), calls=%async_computation.2 | async-start | bytes 1114112 | tf_op jit(solution)/shard_map/all_to_all | solution.py:350
  134.9 21.3 %near.1 = (bf16[16,512,128]{2,1,0:T(8,128)(2,1)}, bf16[16,128,512]{2,1,0:T(8,128)(2,1)}, f32[16,512,128]{2,1,0:T(8,128)}) custom-call(s32[8192]{0:T(1024)} %refs_0_.11, bf16[32,2,256,128]{3,2,1,0:T(8,128)(2,1)} %bitcast.13, bf16[16,512,128]{2,1,0:T(8,128)(2,1)} %rows.1.refs_2_.refs_4_, f32[16,512,128]{2,1,0:T(8,128)} %get-tuple-element.17.refs_3_.refs_5_, ...), custom_call_target="tpu_custom_call" | custom-call | flops 4000000000 | bytes 21004288 | tf_op jit(solution)/shard_map/near/pallas_call | solution.py:24
  156.2 0.8 copy-done.2
  157.0 20.2 %turn.1 = (bf16[16,512,128]{2,1,0:T(8,128)(2,1)}, bf16[16,512,128]{2,1,0:T(8,128)(2,1)}, f32[16,128,128]{2,1,0:T(8,128)}, f32[1,136,128]{2,1,0:T(8,128)}) custom-call(s32[1]{0:T(128)} %bitcast.refs_0_.refs_1_, f32[1]{0:T(128)S(6)} %copy.12.refs_1_.refs_2_, bf16[16,512,128]{2,1,0:T(8,128)(2,1)} %get-tuple-element.20.refs_2_, ...), custom_call_target="tpu_custom_call" | custom-call | flops 2000000000 | bytes 21602312 | tf_op jit(solution)/shard_map/turn/pallas_call | solution.py:24
  177.2 1.8 broadcast_in_dim.41
  179.0 4.8 %all-to-all-start.4 = ((f32[8,136,128]{2,1,0:T(8,128)}), f32[8,136,128]{2,1,0:T(8,128)S(1)}, u32[]{:S(2)}, u32[]{:S(2)}) async-start(f32[8,136,128]{2,1,0:T(8,128)} %broadcast_in_dim.41), calls=%async_computation.4 | async-start | bytes 1114112 | tf_op jit(solution)/shard_map/all_to_all | solution.py:350
  183.8 25.5 %place.1 = (bf16[32,64,256]{2,1,0:T(8,128)(2,1)}, f32[16,512,128]{2,1,0:T(8,128)}) custom-call(s32[8192]{0:T(1024)} %refs_0_.11, bf16[16,512,128]{2,1,0:T(8,128)(2,1)} %get-tuple-element.25.refs_1_, bf16[16,512,128]{2,1,0:T(8,128)(2,1)} %get-tuple-element.26.refs_2_.refs_4_, f32[16,512,128]{2,1,0:T(8,128)} %get-tuple-element.17.refs_3_.refs_5_, ...), custom_call_target="tpu_custom_call" | custom-call | flops 4000000000 | bytes 17858560 | tf_op jit(solution)/shard_map/place/pallas_call | solution.py:24
  209.4 5.6 %all-to-all-start.3 = ((bf16[32,64,256]{2,1,0:T(8,128)(2,1)}), bf16[32,64,256]{2,1,0:T(8,128)(2,1)S(1)}, u32[]{:S(2)}, u32[]{:S(2)}) async-start(bf16[32,64,256]{2,1,0:T(8,128)(2,1)} %get-tuple-element.28), calls=%async_computation.3 | async-start | bytes 2097152 | tf_op jit(solution)/shard_map/all_to_all | solution.py:350
  215.0 25.0 %finish.1 = bf16[32,64,256]{2,1,0:T(8,128)(2,1)} custom-call(s32[8192]{0:T(1024)} %refs_0_.11, s32[1]{0:T(128)} %bitcast.refs_0_.refs_1_, f32[1]{0:T(128)S(6)} %copy.12.refs_1_.refs_2_, bf16[16,512,128]{2,1,0:T(8,128)(2,1)} %get-tuple-element.27.refs_4_.refs_3_, bf16[16,512,128]{2,1,0:T(8,128)(2,1)} %get-tuple-element.26.refs_2_.refs_4_, ...), custom_call_target="tpu_custom_call" | custom-call | flops 2000000000 | bytes 15269896 | tf_op jit(solution)/shard_map/finish/pallas_call | solution.py:24
  240.0 3.1 %all-to-all-done.3 = bf16[32,64,256]{2,1,0:T(8,128)(2,1)S(1)} async-done(((bf16[32,64,256]{2,1,0:T(8,128)(2,1)}), bf16[32,64,256]{2,1,0:T(8,128)(2,1)S(1)}, u32[]{:S(2)}, u32[]{:S(2)}) %all-to-all-start.3) | async-done | bytes 1048608 | tf_op jit(solution)/shard_map/all_to_all | solution.py:350
  243.1 6.7 %all-to-all-start.5 = ((bf16[32,64,256]{2,1,0:T(8,128)(2,1)}), bf16[32,64,256]{2,1,0:T(8,128)(2,1)S(1)}, u32[]{:S(2)}, u32[]{:S(2)}) async-start(bf16[32,64,256]{2,1,0:T(8,128)(2,1)} %finish.1), calls=%async_computation.5 | async-start | bytes 2097152 | tf_op jit(solution)/shard_map/all_to_all | solution.py:350
  249.8 28.2 %all-to-all-done.5 = bf16[32,64,256]{2,1,0:T(8,128)(2,1)S(1)} async-done(((bf16[32,64,256]{2,1,0:T(8,128)(2,1)}), bf16[32,64,256]{2,1,0:T(8,128)(2,1)S(1)}, u32[]{:S(2)}, u32[]{:S(2)}) %all-to-all-start.5) | async-done | bytes 1048608 | tf_op jit(solution)/shard_map/all_to_all | solution.py:350
  278.0 1.0 copy.13
  279.0 1.0 copy.14
  (14 shorter events, 1.5 us)
Async XLA Ops:
  7.2 103.7 %all-gather.3.cloned.1.call-start = ((), (), s32[]{:S(2)}) async-start(), calls=%async_computation.6 | async-start | bytes 4325376 | tf_op jit(solution)/shard_map/all_gather | solution.py:355
  11.1 49.6 %copy-start.3 = (s32[1,8192]{1,0:T(1,128)S(1)}, s32[1,8192]{1,0:T(1,128)}, u32[]{:S(2)}) copy-start(s32[1,8192]{1,0:T(1,128)} %param.12) | copy-start | bytes 98308
  55.1 40.6 %all-to-all-start = ((bf16[32,64,256]{2,1,0:T(8,128)(2,1)}), bf16[32,64,256]{2,1,0:T(8,128)(2,1)S(1)}, u32[]{:S(2)}, u32[]{:S(2)}) async-start(bf16[32,64,256]{2,1,0:T(8,128)(2,1)} %bitcast.4), calls=%async_computation | async-start | bytes 2097152 | tf_op jit(solution)/shard_map/all_to_all | solution.py:350
  95.7 1.0 copy-start
  129.7 26.5 %all-to-all-start.2 = ((f32[8,136,128]{2,1,0:T(8,128)}), f32[8,136,128]{2,1,0:T(8,128)S(1)}, u32[]{:S(2)}, u32[]{:S(2)}) async-start(f32[8,136,128]{2,1,0:T(8,128)} %broadcast_in_dim.39), calls=%async_computation.2 | async-start | bytes 1114112 | tf_op jit(solution)/shard_map/all_to_all | solution.py:350
  156.2 0.8 copy-start.2
  179.0 30.4 %all-to-all-start.4 = ((f32[8,136,128]{2,1,0:T(8,128)}), f32[8,136,128]{2,1,0:T(8,128)S(1)}, u32[]{:S(2)}, u32[]{:S(2)}) async-start(f32[8,136,128]{2,1,0:T(8,128)} %broadcast_in_dim.41), calls=%async_computation.4 | async-start | bytes 1114112 | tf_op jit(solution)/shard_map/all_to_all | solution.py:350
  209.4 5.6 %copy-start.1 = (f32[8,136,128]{2,1,0:T(8,128)}, f32[8,136,128]{2,1,0:T(8,128)S(1)}, u32[]{:S(2)}) copy-start(f32[8,136,128]{2,1,0:T(8,128)S(1)} %all-to-all-done.4.refs_8_) | copy-start | bytes 1671172
  209.4 33.7 %all-to-all-start.3 = ((bf16[32,64,256]{2,1,0:T(8,128)(2,1)}), bf16[32,64,256]{2,1,0:T(8,128)(2,1)S(1)}, u32[]{:S(2)}, u32[]{:S(2)}) async-start(bf16[32,64,256]{2,1,0:T(8,128)(2,1)} %get-tuple-element.28), calls=%async_computation.3 | async-start | bytes 2097152 | tf_op jit(solution)/shard_map/all_to_all | solution.py:350
  243.1 34.9 %all-to-all-start.5 = ((bf16[32,64,256]{2,1,0:T(8,128)(2,1)}), bf16[32,64,256]{2,1,0:T(8,128)(2,1)S(1)}, u32[]{:S(2)}, u32[]{:S(2)}) async-start(bf16[32,64,256]{2,1,0:T(8,128)(2,1)} %finish.1), calls=%async_computation.5 | async-start | bytes 2097152 | tf_op jit(solution)/shard_map/all_to_all | solution.py:350
Sparse Core Ops, SparseCore 0:
  11.1 97.4 all-gather.2
where the time goes:
time: 288 us; the launch traced here: 287 us
  Pallas kernels  146 us (51%)
  waiting for transfers between devices  44.7 us (16%)
  blocking collectives  44 us (15%)
  starting transfers between devices  27.3 us (9%)
  between operations  14.8 us (5%)
  local copies, waits for them, and re-layouts  7.25 us (3%)
    pallas_call x8, Pallas kernels, call(): pl.pallas_call(partial(streaming, kernel, len(scalars), len(arrays), len(...  146 us
    all_to_all x5, waiting for transfers between devices, swap(): return lax.all_to_all(a, axis, split_axis=0, concat_axis=0, tiled=True)  44.6 us
    all_to_all x1, blocking collectives, swap(): return lax.all_to_all(a, axis, split_axis=0, concat_axis=0, tiled=True)  44 us
    all_to_all x5, starting transfers between devices, swap(): return lax.all_to_all(a, axis, split_axis=0, concat_axis=0, tiled=True)  27.3 us
  transfers between devices with their start and end apart: 6, of which 3 were waited for; matrix products, arithmetic and copies ran while one was open for 1% of the time, Pallas kernels for 37%

commit v1 on v0

--- a/solution.py
+++ b/solution.py
@@ -14,19 +14,20 @@
 smem = pl.BlockSpec(memory_space=pltpu.SMEM)
 
 
-def call(kernel, outs, scalars, arrays, scratch, flops, name):
-    args = [*scalars, *arrays]
+def call(kernel, outs, scalars, arrays, scratch, flops, name, order=None):
+    ordered = order is not None
+    args = [*scalars, *([order] if ordered else []), *arrays]
     moved = sum(a.size * a.dtype.itemsize for a in args)
     moved += sum(o.size * o.dtype.itemsize for o in outs)
     held = [pltpu.VMEM(v.shape, v.dtype) for v in [*arrays, *outs]]
     most = max(v.shape[0] for v in [*arrays, *outs])
     sems = pltpu.SemaphoreType.DMA((len(held), most))
     return pl.pallas_call(
-        partial(streaming, kernel, len(scalars), len(arrays), len(outs)),
+        partial(streaming, kernel, len(scalars), ordered, len(arrays), len(outs)),
         out_shape=outs,
-        in_specs=[smem] * len(scalars) + [anywhere] * len(arrays),
+        in_specs=[smem] * len(scalars) + [anywhere] * (ordered + len(arrays)),
         out_specs=[anywhere] * len(outs),
-        scratch_shapes=[*held, sems, *scratch],
+        scratch_shapes=[*(order_scratch(order) if ordered else []), *held, sems, *scratch],
         cost_estimate=pl.CostEstimate(flops=flops, bytes_accessed=moved, transcendentals=0),
         name=name,
     )(*args)
@@ -53,16 +54,43 @@
         self.inward(i).wait()
         return self.near[i]
 
+    def put(self, i, value):
+        self.near[i] = value
+
     def give(self, i, value):
         self.near[i] = value
         self.outward(i).start()
 
 
-def streaming(kernel, n_scalars, n_in, n_out, *refs):
-    scalars, refs = refs[:n_scalars], refs[n_scalars:]
-    far, refs = refs[: n_in + n_out], refs[n_in + n_out :]
-    near, sems, scratch = refs[: n_in + n_out], refs[n_in + n_out], refs[n_in + n_out + 1 :]
-    streams = [Stream(f, n, sems.at[k]) for k, (f, n) in enumerate(zip(far, near))]
+def order_scratch(order):
+    return [pltpu.SMEM(order.shape[1:], jnp.int32)] * 2 + [pltpu.SemaphoreType.DMA((2,))]
+
+
+class Order:
+    def __init__(self, far, near, sems):
+        self.far, self.near, self.sems = far, near, sems
+        self.last = far.shape[0] - 1
+
+    def copy(self, b, k):
+        return pltpu.make_async_copy(self.far.at[jnp.minimum(b, self.last)], self.near[k], self.sems.at[k])
+
+    def row(self, k, i):
+        return self.near[k][i // 128, i % 128]
+
+
+def streaming(kernel, n_scalars, ordered, n_in, n_out, *refs):
+    scalars, refs = list(refs[:n_scalars]), refs[n_scalars:]
+    n = ordered + n_in + n_out
+    far, refs = refs[:n], refs[n:]
+    if ordered:
+        order = Order(far[0], refs[:2], refs[2])
+        far, refs = far[1:], refs[3:]
+        order.copy(0, 0).start()
+        order.copy(1, 1).start()
+        scalars = [order, *scalars]
+    n -= ordered
+    near, sems, scratch = refs[:n], refs[n], refs[n + 1 :]
+    streams = [Stream(f, v, sems.at[k]) for k, (f, v) in enumerate(zip(far, near))]
     for stream in streams[:n_in]:
         stream.each(lambda i, s=stream: s.inward(i).start())
     kernel(*scalars, *streams, *scratch)
@@ -87,49 +115,85 @@
     return high, (value - high.astype(f32)).astype(bf16)
 
 
-def gather_rows(order, b, src, dst):
-    first = b * BLOCK
+def gather_rows(order, k, src, dst):
     for i in range(BLOCK):
-        dst[i // 8, pl.ds(i % 8, 1), :] = src[pl.ds(order[first + i], 1), :]
-
-
-def scatter_rows(order, b, src, dst):
-    first = b * BLOCK
+        dst[i // 8, pl.ds(i % 8, 1), :] = src[pl.ds(order.row(k, i), 1), :]
+
+
+def scatter_rows(order, k, src, dst):
     for i in range(BLOCK):
-        dst[pl.ds(order[first + i], 1), :] = src[i // 8, pl.ds(i % 8, 1), :]
-
-
-def gathered_blocks(order, count, src, bufs, work, init):
+        dst[pl.ds(order.row(k, i), 1), :] = src[i // 8, pl.ds(i % 8, 1), :]
+
+
+def arrive(ins, first):
+    for stream in ins:
+        for k in range(2):
+            stream.inward(first + k).wait()
+
+
+def leave(outs, first):
+    for stream in outs:
+        for k in range(2):
+            stream.outward(first + k).start()
+
+
+def gathered_blocks(order, src, bufs, ins, outs, work, init):
+    order.copy(0, 0).wait()
     gather_rows(order, 0, src, bufs[0])
+    order.copy(2, 0).start()
 
     def pair(i, carry):
-        for k in range(2):
-            b = 2 * i + k
-            block = bufs[k][...].reshape(BLOCK, 128)
-            gather_rows(order, jnp.minimum(b + 1, count - 1), src, bufs[1 - k])
-            carry = work(b, block, carry)
+        b = 2 * i
+        arrive(ins, b)
+        order.copy(b + 1, 1).wait()
+        order.copy(b + 2, 0).wait()
+        block = bufs[0][...].reshape(BLOCK, 128)
+        gather_rows(order, 1, src, bufs[1])
+        carry = work(b, block, carry)
+        block = bufs[1][...].reshape(BLOCK, 128)
+        gather_rows(order, 0, src, bufs[0])
+        carry = work(b + 1, block, carry)
+        order.copy(b + 3, 1).start()
+        order.copy(b + 4, 0).start()
+        leave(outs, b)
         return carry
 
-    return lax.fori_loop(0, count // 2, pair, init)
-
-
-def scattered_blocks(order, count, bufs, dst, work):
+    carry = lax.fori_loop(0, outs[0].count // 2, pair, init)
+    order.copy(0, 0).wait()
+    order.copy(0, 1).wait()
+    return carry
+
+
+def scattered_blocks(order, bufs, dst, ins, outs, work):
     def put(k, value):
         bufs[k][...] = value.reshape(BLOCK // 8, 8, 128)
 
+    arrive(ins, 0)
+    order.copy(0, 0).wait()
     put(0, work(0))
+    scatter_rows(order, 0, bufs[0], dst)
     put(1, work(1))
-    scatter_rows(order, 0, bufs[0], dst)
+    order.copy(2, 0).start()
+    leave(outs, 0)
 
     def pair(i, _):
-        for k in range(2):
-            b = 2 * i + k
-            scatter_rows(order, b - 1, bufs[1 - k], dst)
-            put(k, work(b))
+        b = 2 * i
+        arrive(ins, b)
+        order.copy(b - 1, 1).wait()
+        order.copy(b, 0).wait()
+        scatter_rows(order, 1, bufs[1], dst)
+        put(0, work(b))
+        scatter_rows(order, 0, bufs[0], dst)
+        put(1, work(b + 1))
+        order.copy(b + 1, 1).start()
+        order.copy(b + 2, 0).start()
+        leave(outs, b)
         return 0
 
-    lax.fori_loop(1, count // 2, pair, 0)
-    scatter_rows(order, count - 1, bufs[1], dst)
+    lax.fori_loop(1, ins[0].count // 2, pair, 0)
+    order.copy(0, 1).wait()
+    scatter_rows(order, 1, bufs[1], dst)
+    order.copy(0, 0).wait()
 
 
 def packet_kernel(write, read, out):
@@ -151,10 +215,10 @@
 
     def block(b, code, earlier):
         reach = jnp.dot(tri[...], code.astype(bf16), preferred_element_type=f32) + earlier
-        e_out.give(b, jnp.exp(rate * (reach - 0.5 * total)))
+        e_out.put(b, jnp.exp(rate * (reach - 0.5 * total)))
         return reach[BLOCK - 1 : BLOCK, :]
 
-    gathered_blocks(order, e_out.count, code_all, bufs, block, jnp.zeros((1, 128), f32))
+    gathered_blocks(order, code_all, bufs, [], [e_out], block, jnp.zeros((1, 128), f32))
 
 
 def rows_kernel(order, values, targets, xt_out, xt_all, *bufs):
@@ -169,10 +233,10 @@
     lax.fori_loop(0, values.count, load, 0)
 
     def block(b, rows, _):
-        xt_out.give(b, rows.astype(bf16))
+        xt_out.put(b, rows.astype(bf16))
         return 0
 
-    gathered_blocks(order, xt_out.count, xt_all, bufs, block, 0)
+    gathered_blocks(order, xt_all, bufs, [], [xt_out], block, 0)
 
 
 def block_states(scaled, into_t):
@@ -181,9 +245,16 @@
 
 
 def lower_sum(scaled, from_side, into_t):
-    gram = jnp.dot(from_side, into_t, preferred_element_type=f32)
-    gram = jnp.where(lower_part((BLOCK, BLOCK)), gram, 0.0).astype(bf16)
-    return jnp.dot(gram, scaled.astype(bf16), preferred_element_type=f32)
+    half = BLOCK // 2
+    low = scaled.astype(bf16)
+    top = jnp.dot(from_side[:half], into_t[:, :half], preferred_element_type=f32)
+    end = jnp.dot(from_side[half:], into_t, preferred_element_type=f32)
+    keep = lower_part((half, half))
+    top = jnp.where(keep, top, 0.0).astype(bf16)
+    end = jnp.concatenate([end[:, :half], jnp.where(keep, end[:, half:], 0.0)], axis=1).astype(bf16)
+    top = jnp.dot(top, low[:half], preferred_element_type=f32)
+    end = jnp.dot(end, low, preferred_element_type=f32)
+    return jnp.concatenate([top, end], axis=0)
 
 
 def unpack(sides, side, rows_all):
@@ -206,13 +277,14 @@
 
     def block(b, w, summed):
         w_t = w.T.astype(bf16)
-        w_out.give(b, w.astype(bf16))
-        wt_out.give(b, w_t)
-        p = block_states(doubled(xt_in.take(b)) * e_in.take(b), w_t)
-        p_out.give(b, p)
+        w_out.put(b, w.astype(bf16))
+        wt_out.put(b, w_t)
+        p = block_states(doubled(xt_in[b]) * e_in[b], w_t)
+        p_out.put(b, p)
         return summed + p
 
-    summed = gathered_blocks(order, p_out.count, rows_all, bufs, block, jnp.zeros((128, 128), f32))
+    zero = jnp.zeros((128, 128), f32)
+    summed = gathered_blocks(order, rows_all, bufs, [xt_in, e_in], [w_out, wt_out, p_out], block, zero)
     pay_out.give(0, jnp.concatenate([summed, total.take(0)], axis=0))
 
 
@@ -221,13 +293,12 @@
 
     def block(b, q, _):
         q_low = q.astype(bf16)
-        q_out.give(b, q_low)
-        qt_out.give(b, q.T.astype(bf16))
-        scaled = doubled(xt_in.take(b)) * e_in.take(b)
-        near_out.give(b, lower_sum(scaled, q_low, wt_in.take(b)))
+        q_out.put(b, q_low)
+        qt_out.put(b, q.T.astype(bf16))
+        near_out.put(b, lower_sum(doubled(xt_in[b]) * e_in[b], q_low, wt_in[b]))
         return 0
 
-    gathered_blocks(order, near_out.count, rows_all, bufs, block, 0)
+    gathered_blocks(order, rows_all, bufs, [xt_in, e_in, wt_in], [q_out, qt_out, near_out], block, 0)
 
 
 def prepare(unit, me, p_in, others_in, fr):
@@ -292,31 +363,38 @@
     gain = skip[0]
     left = left_half((BLOCK, 128))
 
+    ins = [from_in, from_t, xt_in, e_in, near_in]
+
     def block(b, summed):
-        e = e_in.take(b)
-        xt = xt_in.take(b).astype(f32)
+        e = e_in[b]
+        xt = xt_in[b].astype(f32)
         tx = pltpu.roll(xt, 64, 1)
         x = jnp.where(left, xt, tx)
         t = jnp.where(left, tx, xt)
-        y = (read_out(from_in.take(b), fr[b], near_in.take(b), e) + gain * x).astype(bf16)
-        y_out.give(b, y)
+        y = (read_out(from_in[b], fr[b], near_in[b], e) + gain * x).astype(bf16)
+        y_out.put(b, y)
         residue = jnp.where(t < 1024.0, y.astype(f32) - t, 0.0).astype(bf16)
-        res_out.give(b, residue)
-        p = block_states(residue.astype(f32) * e, from_t.take(b))
-        p_out.give(b, p)
+        res_out.put(b, residue)
+        p = block_states(residue.astype(f32) * e, from_t[b])
+        p_out.put(b, p)
         return summed + p
 
-    summed = lax.fori_loop(0, p_in.count, block, jnp.zeros((128, 128), f32))
+    def pair(i, summed):
+        arrive(ins, 2 * i)
+        summed = block(2 * i + 1, block(2 * i, summed))
+        leave([y_out, res_out, p_out], 2 * i)
+        return summed
+
+    summed = lax.fori_loop(0, p_in.count // 2, pair, jnp.zeros((128, 128), f32))
     pay_out.give(0, jnp.concatenate([summed, total.take(0)], axis=0))
 
 
 def place_kernel(order, y_in, res_in, e_in, into_in, from_t, out, near_out, y_all, *bufs):
     def block(b):
-        scaled = res_in.take(b).astype(f32) * e_in.take(b)
-        near_out.give(b, lower_sum(scaled, into_in.take(b), from_t.take(b)))
-        return y_in.take(b).astype(f32)
-
-    scattered_blocks(order, near_out.count, bufs, y_all, block)
+        near_out.put(b, lower_sum(res_in[b].astype(f32) * e_in[b], into_in[b], from_t[b]))
+        return y_in[b].astype(f32)
+
+    scattered_blocks(order, bufs, y_all, [y_in, res_in, e_in, into_in, from_t], [near_out], block)
     store_positions(y_all, out)
 
 
@@ -325,10 +403,10 @@
     gain = skip[0]
 
     def block(b):
-        y = read_out(into_in.take(b), fr[b], near_in.take(b), e_in.take(b))
-        return y + gain * res_in.take(b).astype(f32)
-
-    scattered_blocks(order, p_in.count, bufs, y_all, block)
+        y = read_out(into_in[b], fr[b], near_in[b], e_in[b])
+        return y + gain * res_in[b].astype(f32)
+
+    scattered_blocks(order, bufs, y_all, [into_in, res_in, e_in, near_in], [], block)
     store_positions(y_all, out)
 
 
@@ -360,6 +438,7 @@
     head_t = swap(marked.reshape(space_size, width, tok), "space")
     codes = decay_codes.astype(f32).reshape(length // 128, 1, 128)
     where = seq_place.reshape(1).astype(jnp.int32)
+    order = scan_order.reshape(blocks, BLOCK // 128, 128)
 
     by_block = struct((blocks, BLOCK, state), bf16)
     wide = struct((blocks, BLOCK, 128), f32)
@@ -374,31 +453,34 @@
     e, total = call(
         partial(decay_kernel, unit),
         [wide, struct((1, 8, 128), f32)],
-        [scan_order],
+        [],
         [codes],
         [full, pltpu.VMEM((BLOCK, BLOCK), bf16), small, small],
         2 * 10**9,
         "decay",
+        order,
     )
-    xt = call(rows_kernel, [by_block], [scan_order], [head_x, head_t], [full, small, small], 10**9, "rows")[0]
+    xt = call(rows_kernel, [by_block], [], [head_x, head_t], [full, small, small], 10**9, "rows", order)[0]
     w, w_t, p, pay = call(
         states_kernel,
         [by_block, by_block_t, states, payload],
-        [scan_order],
+        [],
         [gathered, xt, e, total],
         [full, small, small],
         2 * 10**9,
         "states",
+        order,
     )
     others = swap(jnp.broadcast_to(pay, (seq_size,) + pay.shape[1:]), "seq")
     q, q_t, near = call(
         near_kernel,
         [by_block, by_block_t, wide],
-        [scan_order],
+        [],
         [gathered, xt, e, w_t],
         [full, small, small],
         4 * 10**9,
         "near",
+        order,
     )
     y, residue, p, pay = call(
         partial(turn_kernel, unit),
@@ -413,21 +495,23 @@
     mixed_heads, near = call(
         place_kernel,
         [heads, wide],
-        [scan_order],
+        [],
         [y, residue, e, w, q_t],
         [full, small, small],
         4 * 10**9,
         "place",
+        order,
     )
     mixed = swap(mixed_heads, "space").reshape(features.shape)
     grads_heads = call(
         partial(finish_kernel, unit),
         [heads],
-        [scan_order, where, skip_gain],
+        [where, skip_gain],
         [w, residue, e, near, p, others],
         [read_states, full, small, small],
         2 * 10**9,
         "finish",
+        order,
     )[0]
     grad_features = swap(grads_heads, "space").reshape(features.shape)
     return (mixed, grad_features)

time: 288 us -> 281 us (0.976)
  Pallas kernels: 146 us -> 136 us
    pallas_call x8, Pallas kernels: 146 us -> 136 us  [call(): pl.pallas_call(partial(streaming, kernel, len(scalars), ordered, len(arra...]
  transfers between devices with their start and end apart: 6 -> 6, of which waited for: 3 -> 3; matrix products, arithmetic and copies ran while one was open for 1% -> 1% of each run, Pallas kernels for 37% -> 36%
where the time goes in v1:
time: 281 us; the launch traced here: 278 us
  Pallas kernels  136 us (48%)
  waiting for transfers between devices  46.2 us (16%)
  blocking collectives  44 us (16%)
  starting transfers between devices  27 us (10%)
  between operations  14.8 us (5%)
  local copies, waits for them, and re-layouts  7.25 us (3%)
    pallas_call x8, Pallas kernels, call(): pl.pallas_call(partial(streaming, kernel, len(scalars), ordered, len(arra...  136 us
    all_to_all x5, waiting for transfers between devices, swap(): return lax.all_to_all(a, axis, split_axis=0, concat_axis=0, tiled=True)  46.1 us
    all_to_all x1, blocking collectives, swap(): return lax.all_to_all(a, axis, split_axis=0, concat_axis=0, tiled=True)  44 us
    all_to_all x5, starting transfers between devices, swap(): return lax.all_to_all(a, axis, split_axis=0, concat_axis=0, tiled=True)  26.9 us
  transfers between devices with their start and end apart: 6, of which 3 were waited for; matrix products, arithmetic and copies ran while one was open for 1% of the time, Pallas kernels for 36%

profile of v1, /device:TPU:2, one launch (start us, length us, event | category | flops | bytes accessed | tf_op | source)
XLA Modules:
  0.0 278.2 jit_solution(7776262145950105174)
XLA Ops:
  7.2 1.7 packet.1
  9.8 1.3 broadcast_select_fusion
  11.1 44.0 %all_to_all.30.refs_2_ = bf16[32,64,256]{2,1,0:T(8,128)(2,1)} all-to-all(bf16[32,64,256]{2,1,0:T(8,128)(2,1)S(1)} %bitcast.15), channel_id=1, replica_groups=mesh['seq'=8,'space'=32] {'space'}, dimensions={0} | all-to-all | bytes 2097152 | tf_op jit(solution)/shard_map/all_to_all | solution.py:428
  55.1 5.6 %all-to-all-start = ((bf16[32,64,256]{2,1,0:T(8,128)(2,1)}), bf16[32,64,256]{2,1,0:T(8,128)(2,1)S(1)}, u32[]{:S(2)}, u32[]{:S(2)}) async-start(bf16[32,64,256]{2,1,0:T(8,128)(2,1)} %bitcast.5), calls=%async_computation | async-start | bytes 2097152 | tf_op jit(solution)/shard_map/all_to_all | solution.py:428
  61.3 21.4 %decay.1 = (f32[16,512,128]{2,1,0:T(8,128)}, f32[1,8,128]{2,1,0:T(8,128)}) custom-call(s32[16,4,128]{2,1,0:T(4,128)} %bitcast.18, f32[64,1,128]{2,1,0:T(1,128)} %convert_bitcast_fusion.refs_1_), custom_call_target="tpu_custom_call" | custom-call | flops 2000000000 | bytes 4263936 | tf_op jit(solution)/shard_map/decay/pallas_call | solution.py:25
  82.8 13.0 %all-to-all-done.refs_1_ = bf16[32,64,256]{2,1,0:T(8,128)(2,1)S(1)} async-done(((bf16[32,64,256]{2,1,0:T(8,128)(2,1)}), bf16[32,64,256]{2,1,0:T(8,128)(2,1)S(1)}, u32[]{:S(2)}, u32[]{:S(2)}) %all-to-all-start) | async-done | bytes 1048608 | tf_op jit(solution)/shard_map/all_to_all | solution.py:428
  95.7 1.0 copy-done
  96.7 16.9 %rows.1.refs_2_.refs_4_ = bf16[16,512,128]{2,1,0:T(8,128)(2,1)} custom-call(s32[16,4,128]{2,1,0:T(4,128)} %bitcast.19, bf16[32,64,256]{2,1,0:T(8,128)(2,1)} %copy-done, bf16[32,64,256]{2,1,0:T(8,128)(2,1)} %all_to_all.30.refs_2_), custom_call_target="tpu_custom_call" | custom-call | flops 1000000000 | bytes 4227072 | tf_op jit(solution)/shard_map/rows/pallas_call | solution.py:25
  113.6 18.3 %states.1 = (bf16[16,512,128]{2,1,0:T(8,128)(2,1)}, bf16[16,128,512]{2,1,0:T(8,128)(2,1)}, f32[16,128,128]{2,1,0:T(8,128)}, f32[1,136,128]{2,1,0:T(8,128)}) custom-call(s32[16,4,128]{2,1,0:T(4,128)} %bitcast.20, bf16[32,2,256,128]{3,2,1,0:T(8,128)(2,1)} %bitcast.13, bf16[16,512,128]{2,1,0:T(8,128)(2,1)} %rows.1.refs_2_.refs_4_, ...), custom_call_target="tpu_custom_call" | custom-call | flops 2000000000 | bytes 15835136 | tf_op jit(solution)/shard_map/states/pallas_call | solution.py:25
  131.9 1.7 broadcast_in_dim.39
  133.6 4.6 %all-to-all-start.2 = ((f32[8,136,128]{2,1,0:T(8,128)}), f32[8,136,128]{2,1,0:T(8,128)S(1)}, u32[]{:S(2)}, u32[]{:S(2)}) async-start(f32[8,136,128]{2,1,0:T(8,128)} %broadcast_in_dim.39), calls=%async_computation.2 | async-start | bytes 1114112 | tf_op jit(solution)/shard_map/all_to_all | solution.py:428
  138.8 18.5 %near.1 = (bf16[16,512,128]{2,1,0:T(8,128)(2,1)}, bf16[16,128,512]{2,1,0:T(8,128)(2,1)}, f32[16,512,128]{2,1,0:T(8,128)}) custom-call(s32[16,4,128]{2,1,0:T(4,128)} %bitcast.21, bf16[32,2,256,128]{3,2,1,0:T(8,128)(2,1)} %bitcast.14, bf16[16,512,128]{2,1,0:T(8,128)(2,1)} %rows.1.refs_2_.refs_4_, f32[16,512,128]{2,1,0:T(8,128)} %get-tuple-element.17.refs_3_.refs_5_, ...), custom_call_target="tpu_custom_call" | custom-call | flops 4000000000 | bytes 21004288 | tf_op jit(solution)/shard_map/near/pallas_call | solution.py:25
  157.3 0.8 copy-done.2
  158.1 16.2 %turn.1 = (bf16[16,512,128]{2,1,0:T(8,128)(2,1)}, bf16[16,512,128]{2,1,0:T(8,128)(2,1)}, f32[16,128,128]{2,1,0:T(8,128)}, f32[1,136,128]{2,1,0:T(8,128)}) custom-call(s32[1]{0:T(128)} %bitcast.1.refs_0_, f32[1]{0:T(128)S(6)} %copy.12.refs_1_, bf16[16,512,128]{2,1,0:T(8,128)(2,1)} %get-tuple-element.20.refs_2_, ...), custom_call_target="tpu_custom_call" | custom-call | flops 2000000000 | bytes 21602312 | tf_op jit(solution)/shard_map/turn/pallas_call | solution.py:25
  174.3 1.8 broadcast_in_dim.41
  176.1 4.8 %all-to-all-start.4 = ((f32[8,136,128]{2,1,0:T(8,128)}), f32[8,136,128]{2,1,0:T(8,128)S(1)}, u32[]{:S(2)}, u32[]{:S(2)}) async-start(f32[8,136,128]{2,1,0:T(8,128)} %broadcast_in_dim.41), calls=%async_computation.4 | async-start | bytes 1114112 | tf_op jit(solution)/shard_map/all_to_all | solution.py:428
  180.9 21.0 %place.1 = (bf16[32,64,256]{2,1,0:T(8,128)(2,1)}, f32[16,512,128]{2,1,0:T(8,128)}) custom-call(s32[16,4,128]{2,1,0:T(4,128)} %bitcast.22, bf16[16,512,128]{2,1,0:T(8,128)(2,1)} %get-tuple-element.25.refs_1_, bf16[16,512,128]{2,1,0:T(8,128)(2,1)} %get-tuple-element.26.refs_2_.refs_4_, f32[16,512,128]{2,1,0:T(8,128)} %get-tuple-element.17.refs_3_.refs_5_, ...), custom_call_target="tpu_custom_call" | custom-call | flops 4000000000 | bytes 17858560 | tf_op jit(solution)/shard_map/place/pallas_call | solution.py:25
  201.9 5.8 %all-to-all-start.3 = ((bf16[32,64,256]{2,1,0:T(8,128)(2,1)}), bf16[32,64,256]{2,1,0:T(8,128)(2,1)S(1)}, u32[]{:S(2)}, u32[]{:S(2)}) async-start(bf16[32,64,256]{2,1,0:T(8,128)(2,1)} %get-tuple-element.28), calls=%async_computation.3 | async-start | bytes 2097152 | tf_op jit(solution)/shard_map/all_to_all | solution.py:428
  207.7 22.3 %finish.1 = bf16[32,64,256]{2,1,0:T(8,128)(2,1)} custom-call(s32[1]{0:T(128)} %bitcast.1.refs_0_, f32[1]{0:T(128)S(6)} %copy.12.refs_1_, s32[16,4,128]{2,1,0:T(4,128)} %bitcast.23, bf16[16,512,128]{2,1,0:T(8,128)(2,1)} %get-tuple-element.27.refs_4_.refs_3_, bf16[16,512,128]{2,1,0:T(8,128)(2,1)} %get-tuple-element.26.refs_2_.refs_4_, ...), custom_call_target="tpu_custom_call" | custom-call | flops 2000000000 | bytes 15269896 | tf_op jit(solution)/shard_map/finish/pallas_call | solution.py:25
  230.0 5.8 %all-to-all-done.3 = bf16[32,64,256]{2,1,0:T(8,128)(2,1)S(1)} async-done(((bf16[32,64,256]{2,1,0:T(8,128)(2,1)}), bf16[32,64,256]{2,1,0:T(8,128)(2,1)S(1)}, u32[]{:S(2)}, u32[]{:S(2)}) %all-to-all-start.3) | async-done | bytes 1048608 | tf_op jit(solution)/shard_map/all_to_all | solution.py:428
  235.8 6.2 %all-to-all-start.5 = ((bf16[32,64,256]{2,1,0:T(8,128)(2,1)}), bf16[32,64,256]{2,1,0:T(8,128)(2,1)S(1)}, u32[]{:S(2)}, u32[]{:S(2)}) async-start(bf16[32,64,256]{2,1,0:T(8,128)(2,1)} %finish.1), calls=%async_computation.5 | async-start | bytes 2097152 | tf_op jit(solution)/shard_map/all_to_all | solution.py:428
  242.0 27.4 %all-to-all-done.5 = bf16[32,64,256]{2,1,0:T(8,128)(2,1)S(1)} async-done(((bf16[32,64,256]{2,1,0:T(8,128)(2,1)}), bf16[32,64,256]{2,1,0:T(8,128)(2,1)S(1)}, u32[]{:S(2)}, u32[]{:S(2)}) %all-to-all-start.5) | async-done | bytes 1048608 | tf_op jit(solution)/shard_map/all_to_all | solution.py:428
  269.4 1.0 copy.13
  270.3 1.0 copy.14
  (14 shorter events, 1.5 us)
Async XLA Ops:
  7.2 106.4 %all-gather.3.cloned.1.call-start = ((), (), s32[]{:S(2)}) async-start(), calls=%async_computation.6 | async-start | bytes 4325376 | tf_op jit(solution)/shard_map/all_gather | solution.py:433
  11.1 49.6 %copy-start.3 = (s32[1,8192]{1,0:T(1,128)S(1)}, s32[1,8192]{1,0:T(1,128)}, u32[]{:S(2)}) copy-start(s32[1,8192]{1,0:T(1,128)} %param.12) | copy-start | bytes 98308
  55.1 40.6 %all-to-all-start = ((bf16[32,64,256]{2,1,0:T(8,128)(2,1)}), bf16[32,64,256]{2,1,0:T(8,128)(2,1)S(1)}, u32[]{:S(2)}, u32[]{:S(2)}) async-start(bf16[32,64,256]{2,1,0:T(8,128)(2,1)} %bitcast.5), calls=%async_computation | async-start | bytes 2097152 | tf_op jit(solution)/shard_map/all_to_all | solution.py:428
  95.7 1.0 copy-start
  133.6 23.7 %all-to-all-start.2 = ((f32[8,136,128]{2,1,0:T(8,128)}), f32[8,136,128]{2,1,0:T(8,128)S(1)}, u32[]{:S(2)}, u32[]{:S(2)}) async-start(f32[8,136,128]{2,1,0:T(8,128)} %broadcast_in_dim.39), calls=%async_computation.2 | async-start | bytes 1114112 | tf_op jit(solution)/shard_map/all_to_all | solution.py:428
  157.3 0.8 copy-start.2
  176.1 25.8 %all-to-all-start.4 = ((f32[8,136,128]{2,1,0:T(8,128)}), f32[8,136,128]{2,1,0:T(8,128)S(1)}, u32[]{:S(2)}, u32[]{:S(2)}) async-start(f32[8,136,128]{2,1,0:T(8,128)} %broadcast_in_dim.41), calls=%async_computation.4 | async-start | bytes 1114112 | tf_op jit(solution)/shard_map/all_to_all | solution.py:428
  201.9 5.8 %copy-start.1 = (f32[8,136,128]{2,1,0:T(8,128)}, f32[8,136,128]{2,1,0:T(8,128)S(1)}, u32[]{:S(2)}) copy-start(f32[8,136,128]{2,1,0:T(8,128)S(1)} %all-to-all-done.4.refs_8_) | copy-start | bytes 1671172
  201.9 33.9 %all-to-all-start.3 = ((bf16[32,64,256]{2,1,0:T(8,128)(2,1)}), bf16[32,64,256]{2,1,0:T(8,128)(2,1)S(1)}, u32[]{:S(2)}, u32[]{:S(2)}) async-start(bf16[32,64,256]{2,1,0:T(8,128)(2,1)} %get-tuple-element.28), calls=%async_computation.3 | async-start | bytes 2097152 | tf_op jit(solution)/shard_map/all_to_all | solution.py:428
  235.8 33.6 %all-to-all-start.5 = ((bf16[32,64,256]{2,1,0:T(8,128)(2,1)}), bf16[32,64,256]{2,1,0:T(8,128)(2,1)S(1)}, u32[]{:S(2)}, u32[]{:S(2)}) async-start(bf16[32,64,256]{2,1,0:T(8,128)(2,1)} %finish.1), calls=%async_computation.5 | async-start | bytes 2097152 | tf_op jit(solution)/shard_map/all_to_all | solution.py:428
Sparse Core Ops, SparseCore 0:
  11.1 97.4 all-gather.2

commit v2 on v1

--- a/solution.py
+++ b/solution.py
@@ -221,22 +221,29 @@
     gathered_blocks(order, code_all, bufs, [], [e_out], block, jnp.zeros((1, 128), f32))
 
 
-def rows_kernel(order, values, targets, xt_out, xt_all, *bufs):
-    tok = values.shape[2]
+def rows_kernel(places, xt_in, xt_out, xt_all, rows):
+    tok = xt_in.shape[2]
 
     def load(c, _):
         base = pl.multiple_of(c * tok, tok)
-        both = jnp.concatenate([values.take(c).astype(f32), targets.take(c).astype(f32)], axis=0)
-        xt_all[pl.ds(base, tok), :] = both.T
+        xt_all[pl.ds(base, tok), :] = xt_in.take(c).astype(f32).T
         return 0
 
-    lax.fori_loop(0, values.count, load, 0)
-
-    def block(b, rows, _):
-        xt_out.put(b, rows.astype(bf16))
+    lax.fori_loop(0, xt_in.count, load, 0)
+
+    def block(b, _):
+        def some(j, _):
+            row = places.at[b * (BLOCK // 128) + j]
+            part = rows.at[pl.ds(j * 16, 16)]
+            for i in range(128):
+                part[i // 8, pl.ds(i % 8, 1), :] = xt_all[pl.ds(row[i], 1), :]
+            return 0
+
+        lax.fori_loop(0, BLOCK // 128, some, 0)
+        xt_out.give(b, rows[...].reshape(BLOCK, 128).astype(bf16))
         return 0
 
-    gathered_blocks(order, xt_all, bufs, [], [xt_out], block, 0)
+    lax.fori_loop(0, xt_out.count, block, 0)
 
 
 def block_states(scaled, into_t):
@@ -285,7 +292,9 @@
 
     zero = jnp.zeros((128, 128), f32)
     summed = gathered_blocks(order, rows_all, bufs, [xt_in, e_in], [w_out, wt_out, p_out], block, zero)
-    pay_out.give(0, jnp.concatenate([summed, total.take(0)], axis=0))
+    pay = jnp.concatenate([summed, total.take(0)], axis=0)
+    for g in range(pay_out.count):
+        pay_out.give(g, pay)
 
 
 def near_kernel(order, read, xt_in, e_in, wt_in, q_out, qt_out, near_out, rows_all, *bufs):
@@ -386,7 +395,9 @@
         return summed
 
     summed = lax.fori_loop(0, p_in.count // 2, pair, jnp.zeros((128, 128), f32))
-    pay_out.give(0, jnp.concatenate([summed, total.take(0)], axis=0))
+    pay = jnp.concatenate([summed, total.take(0)], axis=0)
+    for g in range(pay_out.count):
+        pay_out.give(g, pay)
 
 
 def place_kernel(order, y_in, res_in, e_in, into_in, from_t, out, near_out, y_all, *bufs):
@@ -431,11 +442,11 @@
         packet_kernel, [struct((2, tok, state), bf16)], [], [write_keys[None], read_queries[None]], [], 0, "packet"
     )[0]
     gathered = lax.all_gather(packet, "space", axis=0, tiled=False)
-    head_x = swap(features.reshape(space_size, width, tok), "space")
     slot_grid = lax.broadcasted_iota(jnp.int32, (masked.shape[0], tok), 1)
     is_masked = jnp.any((masked - first_token)[:, None] == slot_grid, axis=0)
     marked = jnp.where(is_masked[None], targets, jnp.asarray(MARK, bf16))
-    head_t = swap(marked.reshape(space_size, width, tok), "space")
+    both = [a.reshape(space_size, width, tok) for a in (features, marked)]
+    head_xt = swap(jnp.concatenate(both, axis=1), "space")
     codes = decay_codes.astype(f32).reshape(length // 128, 1, 128)
     where = seq_place.reshape(1).astype(jnp.int32)
     order = scan_order.reshape(blocks, BLOCK // 128, 128)
@@ -444,7 +455,7 @@
     wide = struct((blocks, BLOCK, 128), f32)
     by_block_t = struct((blocks, state, BLOCK), bf16)
     states = struct((blocks, state, 128), f32)
-    payload = struct((1, state + 8, 128), f32)
+    payload = struct((seq_size, state + 8, 128), f32)
     heads = struct((space_size, width, tok), bf16)
     small = pltpu.VMEM((BLOCK // 8, 8, 128), f32)
     full = pltpu.VMEM((length, 128), f32)
@@ -460,7 +471,8 @@
         "decay",
         order,
     )
-    xt = call(rows_kernel, [by_block], [], [head_x, head_t], [full, small, small], 10**9, "rows", order)[0]
+    places = scan_order.reshape(length // 128, 128)
+    xt = call(rows_kernel, [by_block], [places], [head_xt], [full, small], 10**9, "rows")[0]
     w, w_t, p, pay = call(
         states_kernel,
         [by_block, by_block_t, states, payload],
@@ -471,7 +483,7 @@
         "states",
         order,
     )
-    others = swap(jnp.broadcast_to(pay, (seq_size,) + pay.shape[1:]), "seq")
+    others = swap(pay, "seq")
     q, q_t, near = call(
         near_kernel,
         [by_block, by_block_t, wide],
@@ -491,7 +503,7 @@
         2 * 10**9,
         "turn",
     )
-    others = swap(jnp.broadcast_to(pay, (seq_size,) + pay.shape[1:]), "seq")
+    others = swap(pay, "seq")
     mixed_heads, near = call(
         place_kernel,
         [heads, wide],

time: 281 us -> 268 us (0.954)
  blocking collectives: 44 us -> 0 us
  waiting for transfers between devices: 46.2 us -> 74.5 us
  starting transfers between devices: 27 us -> 35.1 us
  local copies, waits for them, and re-layouts: 7.25 us -> 4.17 us
  Pallas kernels: 136 us -> 133 us
    all_to_all x1 -> x0, blocking collectives: 44 us -> none  [swap(): return lax.all_to_all(a, axis, split_axis=0, concat_axis=0, tiled=True)]
    all_to_all x5, waiting for transfers between devices: 46.1 us -> 68.9 us  [swap(): return lax.all_to_all(a, axis, split_axis=0, concat_axis=0, tiled=True)]
    all_to_all x5, starting transfers between devices: 26.9 us -> 35.1 us  [swap(): return lax.all_to_all(a, axis, split_axis=0, concat_axis=0, tiled=True)]
    all_gather x1, waiting for transfers between devices: 0.02 us -> 5.57 us  [per_device(): gathered = lax.all_gather(packet, 'space', axis=0, tiled=False)]
    broadcast_in_dim x2 -> x0, local copies, waits for them, and re-layouts: 3.52 us -> none  [per_device(): others = swap(jnp.broadcast_to(pay, (seq_size,) + pay.shape[1:]), 'seq')]
    pallas_call x8, Pallas kernels: 136 us -> 133 us  [call(): pl.pallas_call(partial(streaming, kernel, len(scalars), ordered, len(arra...]
  transfers between devices with their start and end apart: 6 -> 6, of which waited for: 3 -> 4; matrix products, arithmetic and copies ran while one was open for 1% -> 2% of each run, Pallas kernels for 36% -> 36%
where the time goes in v2:
time: 268 us; the launch traced here: 266 us
  Pallas kernels  133 us (50%)
  waiting for transfers between devices  74.5 us (28%)
  starting transfers between devices  35.1 us (13%)
  between operations  14.8 us (6%)
  other arithmetic  4.28 us (2%)
  local copies, waits for them, and re-layouts  4.17 us (2%)
    pallas_call x8, Pallas kernels, call(): pl.pallas_call(partial(streaming, kernel, len(scalars), ordered, len(arra...  133 us
    all_to_all x5, waiting for transfers between devices, swap(): return lax.all_to_all(a, axis, split_axis=0, concat_axis=0, tiled=True)  68.9 us
    all_to_all x5, starting transfers between devices, swap(): return lax.all_to_all(a, axis, split_axis=0, concat_axis=0, tiled=True)  35.1 us
    all_gather x1, waiting for transfers between devices, per_device(): gathered = lax.all_gather(packet, 'space', axis=0, tiled=False)  5.57 us
  transfers between devices with their start and end apart: 6, of which 4 were waited for; matrix products, arithmetic and copies ran while one was open for 2% of the time, Pallas kernels for 36%

profile of v2, /device:TPU:2, one launch (start us, length us, event | category | flops | bytes accessed | tf_op | source)
XLA Modules:
  0.0 266.2 jit_solution(11161114762610135287)
XLA Ops:
  7.2 1.8 packet.1
  9.1 0.7 broadcast_subtract_fusion
  9.9 1.3 broadcast_select_fusion
  11.2 1.5 pad_maximum_fusion
  12.7 11.7 %all-to-all-start = ((bf16[32,128,256]{2,1,0:T(8,128)(2,1)}), bf16[32,128,256]{2,1,0:T(8,128)(2,1)S(1)}, u32[]{:S(2)}, u32[]{:S(2)}) async-start(bf16[32,128,256]{2,1,0:T(8,128)(2,1)} %pad_maximum_fusion), calls=%async_computation | async-start | bytes 4194304 | tf_op jit(solution)/shard_map/all_to_all | solution.py:439
  25.1 21.4 %decay.1 = (f32[16,512,128]{2,1,0:T(8,128)}, f32[1,8,128]{2,1,0:T(8,128)}) custom-call(s32[16,4,128]{2,1,0:T(4,128)} %bitcast.18, f32[64,1,128]{2,1,0:T(1,128)} %convert_bitcast_fusion.refs_1_), custom_call_target="tpu_custom_call" | custom-call | flops 2000000000 | bytes 4263936 | tf_op jit(solution)/shard_map/decay/pallas_call | solution.py:25
  46.6 35.7 %all-to-all-done.refs_1_ = bf16[32,128,256]{2,1,0:T(8,128)(2,1)S(1)} async-done(((bf16[32,128,256]{2,1,0:T(8,128)(2,1)}), bf16[32,128,256]{2,1,0:T(8,128)(2,1)S(1)}, u32[]{:S(2)}, u32[]{:S(2)}) %all-to-all-start) | async-done | bytes 2097184 | tf_op jit(solution)/shard_map/all_to_all | solution.py:439
  82.3 1.3 copy-done
  83.7 13.7 %rows.1.refs_2_.refs_4_ = bf16[16,512,128]{2,1,0:T(8,128)(2,1)} custom-call(s32[64,128]{1,0:T(8,128)} %bitcast.19, bf16[32,128,256]{2,1,0:T(8,128)(2,1)} %copy-done), custom_call_target="tpu_custom_call" | custom-call | flops 1000000000 | bytes 4227072 | tf_op jit(solution)/shard_map/rows/pallas_call | solution.py:25
  97.4 5.6 %all-gather.3.cloned.1.call-done = bf16[64,256,128]{2,1,0:T(8,128)(2,1)} async-done(((bf16[2,256,128]{2,1,0:T(8,128)(2,1)}), bf16[64,256,128]{2,1,0:T(8,128)(2,1)}) %all-gather.3.cloned.1.call-update) | async-done | bytes 4194320 | tf_op jit(solution)/shard_map/all_gather | solution.py:444
  102.9 18.4 %states.1 = (bf16[16,512,128]{2,1,0:T(8,128)(2,1)}, bf16[16,128,512]{2,1,0:T(8,128)(2,1)}, f32[16,128,128]{2,1,0:T(8,128)}, f32[8,136,128]{2,1,0:T(8,128)}) custom-call(s32[16,4,128]{2,1,0:T(4,128)} %bitcast.20, bf16[32,2,256,128]{3,2,1,0:T(8,128)(2,1)} %bitcast.12, bf16[16,512,128]{2,1,0:T(8,128)(2,1)} %rows.1.refs_2_.refs_4_, ...), custom_call_target="tpu_custom_call" | custom-call | flops 2000000000 | bytes 16322560 | tf_op jit(solution)/shard_map/states/pallas_call | solution.py:25
  121.3 4.5 %all-to-all-start.1 = ((f32[8,136,128]{2,1,0:T(8,128)}), f32[8,136,128]{2,1,0:T(8,128)S(1)}, u32[]{:S(2)}, u32[]{:S(2)}) async-start(f32[8,136,128]{2,1,0:T(8,128)} %get-tuple-element.24), calls=%async_computation.1 | async-start | bytes 1114112 | tf_op jit(solution)/shard_map/all_to_all | solution.py:439
  126.4 18.5 %near.1 = (bf16[16,512,128]{2,1,0:T(8,128)(2,1)}, bf16[16,128,512]{2,1,0:T(8,128)(2,1)}, f32[16,512,128]{2,1,0:T(8,128)}) custom-call(s32[16,4,128]{2,1,0:T(4,128)} %bitcast.21, bf16[32,2,256,128]{3,2,1,0:T(8,128)(2,1)} %bitcast.13, bf16[16,512,128]{2,1,0:T(8,128)(2,1)} %rows.1.refs_2_.refs_4_, f32[16,512,128]{2,1,0:T(8,128)} %get-tuple-element.17.refs_3_.refs_5_, ...), custom_call_target="tpu_custom_call" | custom-call | flops 4000000000 | bytes 21004288 | tf_op jit(solution)/shard_map/near/pallas_call | solution.py:25
  145.0 0.9 copy-done.2
  145.8 16.2 %turn.1 = (bf16[16,512,128]{2,1,0:T(8,128)(2,1)}, bf16[16,512,128]{2,1,0:T(8,128)(2,1)}, f32[16,128,128]{2,1,0:T(8,128)}, f32[8,136,128]{2,1,0:T(8,128)}) custom-call(s32[1]{0:T(128)} %bitcast.1.refs_0_, f32[1]{0:T(128)S(6)} %copy.12.refs_1_, bf16[16,512,128]{2,1,0:T(8,128)(2,1)} %get-tuple-element.20.refs_2_, ...), custom_call_target="tpu_custom_call" | custom-call | flops 2000000000 | bytes 22089736 | tf_op jit(solution)/shard_map/turn/pallas_call | solution.py:25
  162.1 4.8 %all-to-all-start.3 = ((f32[8,136,128]{2,1,0:T(8,128)}), f32[8,136,128]{2,1,0:T(8,128)S(1)}, u32[]{:S(2)}, u32[]{:S(2)}) async-start(f32[8,136,128]{2,1,0:T(8,128)} %get-tuple-element.31), calls=%async_computation.3 | async-start | bytes 1114112 | tf_op jit(solution)/shard_map/all_to_all | solution.py:439
  166.9 21.0 %place.1 = (bf16[32,64,256]{2,1,0:T(8,128)(2,1)}, f32[16,512,128]{2,1,0:T(8,128)}) custom-call(s32[16,4,128]{2,1,0:T(4,128)} %bitcast.22, bf16[16,512,128]{2,1,0:T(8,128)(2,1)} %get-tuple-element.25.refs_1_, bf16[16,512,128]{2,1,0:T(8,128)(2,1)} %get-tuple-element.26.refs_2_.refs_4_, f32[16,512,128]{2,1,0:T(8,128)} %get-tuple-element.17.refs_3_.refs_5_, ...), custom_call_target="tpu_custom_call" | custom-call | flops 4000000000 | bytes 17858560 | tf_op jit(solution)/shard_map/place/pallas_call | solution.py:25
  187.9 7.8 %all-to-all-start.2 = ((bf16[32,64,256]{2,1,0:T(8,128)(2,1)}), bf16[32,64,256]{2,1,0:T(8,128)(2,1)S(1)}, u32[]{:S(2)}, u32[]{:S(2)}) async-start(bf16[32,64,256]{2,1,0:T(8,128)(2,1)} %get-tuple-element.28), calls=%async_computation.2 | async-start | bytes 2097152 | tf_op jit(solution)/shard_map/all_to_all | solution.py:439
  195.8 22.3 %finish.1 = bf16[32,64,256]{2,1,0:T(8,128)(2,1)} custom-call(s32[1]{0:T(128)} %bitcast.1.refs_0_, f32[1]{0:T(128)S(6)} %copy.12.refs_1_, s32[16,4,128]{2,1,0:T(4,128)} %bitcast.23, bf16[16,512,128]{2,1,0:T(8,128)(2,1)} %get-tuple-element.27.refs_4_.refs_3_, bf16[16,512,128]{2,1,0:T(8,128)(2,1)} %get-tuple-element.26.refs_2_.refs_4_, ...), custom_call_target="tpu_custom_call" | custom-call | flops 2000000000 | bytes 15269896 | tf_op jit(solution)/shard_map/finish/pallas_call | solution.py:25
  218.1 5.8 %all-to-all-done.2 = bf16[32,64,256]{2,1,0:T(8,128)(2,1)S(1)} async-done(((bf16[32,64,256]{2,1,0:T(8,128)(2,1)}), bf16[32,64,256]{2,1,0:T(8,128)(2,1)S(1)}, u32[]{:S(2)}, u32[]{:S(2)}) %all-to-all-start.2) | async-done | bytes 1048608 | tf_op jit(solution)/shard_map/all_to_all | solution.py:439
  223.8 6.2 %all-to-all-start.4 = ((bf16[32,64,256]{2,1,0:T(8,128)(2,1)}), bf16[32,64,256]{2,1,0:T(8,128)(2,1)S(1)}, u32[]{:S(2)}, u32[]{:S(2)}) async-start(bf16[32,64,256]{2,1,0:T(8,128)(2,1)} %finish.1), calls=%async_computation.4 | async-start | bytes 2097152 | tf_op jit(solution)/shard_map/all_to_all | solution.py:439
  230.0 27.4 %all-to-all-done.4 = bf16[32,64,256]{2,1,0:T(8,128)(2,1)S(1)} async-done(((bf16[32,64,256]{2,1,0:T(8,128)(2,1)}), bf16[32,64,256]{2,1,0:T(8,128)(2,1)S(1)}, u32[]{:S(2)}, u32[]{:S(2)}) %all-to-all-start.4) | async-done | bytes 1048608 | tf_op jit(solution)/shard_map/all_to_all | solution.py:439
  257.4 1.0 copy.13
  258.4 1.0 copy.14
  (14 shorter events, 0.8 us)
Async XLA Ops:
  7.2 4.0 %copy-start.3 = (bf16[2048,256]{1,0:T(8,128)(2,1)S(1)}, bf16[2048,256]{1,0:T(8,128)(2,1)}, u32[]{:S(2)}) copy-start(bf16[2048,256]{1,0:T(8,128)(2,1)} %param.8) | copy-start | bytes 3145732
  7.2 95.8 %all-gather.3.cloned.1.call-start = ((), (), s32[]{:S(2)}) async-start(), calls=%async_computation.5 | async-start | bytes 4325376 | tf_op jit(solution)/shard_map/all_gather | solution.py:444
  12.7 11.8 %copy-start.4 = (s32[1,8192]{1,0:T(1,128)S(1)}, s32[1,8192]{1,0:T(1,128)}, u32[]{:S(2)}) copy-start(s32[1,8192]{1,0:T(1,128)} %param.12) | copy-start | bytes 98308
  12.7 69.6 %all-to-all-start = ((bf16[32,128,256]{2,1,0:T(8,128)(2,1)}), bf16[32,128,256]{2,1,0:T(8,128)(2,1)S(1)}, u32[]{:S(2)}, u32[]{:S(2)}) async-start(bf16[32,128,256]{2,1,0:T(8,128)(2,1)} %pad_maximum_fusion), calls=%async_computation | async-start | bytes 4194304 | tf_op jit(solution)/shard_map/all_to_all | solution.py:439
  82.3 1.3 copy-start
  121.3 23.6 %all-to-all-start.1 = ((f32[8,136,128]{2,1,0:T(8,128)}), f32[8,136,128]{2,1,0:T(8,128)S(1)}, u32[]{:S(2)}, u32[]{:S(2)}) async-start(f32[8,136,128]{2,1,0:T(8,128)} %get-tuple-element.24), calls=%async_computation.1 | async-start | bytes 1114112 | tf_op jit(solution)/shard_map/all_to_all | solution.py:439
  144.9 0.9 copy-start.2
  162.1 25.8 %all-to-all-start.3 = ((f32[8,136,128]{2,1,0:T(8,128)}), f32[8,136,128]{2,1,0:T(8,128)S(1)}, u32[]{:S(2)}, u32[]{:S(2)}) async-start(f32[8,136,128]{2,1,0:T(8,128)} %get-tuple-element.31), calls=%async_computation.3 | async-start | bytes 1114112 | tf_op jit(solution)/shard_map/all_to_all | solution.py:439
  187.9 7.9 %copy-start.1 = (f32[8,136,128]{2,1,0:T(8,128)}, f32[8,136,128]{2,1,0:T(8,128)S(1)}, u32[]{:S(2)}) copy-start(f32[8,136,128]{2,1,0:T(8,128)S(1)} %all-to-all-done.3.refs_8_) | copy-start | bytes 1671172
  187.9 35.9 %all-to-all-start.2 = ((bf16[32,64,256]{2,1,0:T(8,128)(2,1)}), bf16[32,64,256]{2,1,0:T(8,128)(2,1)S(1)}, u32[]{:S(2)}, u32[]{:S(2)}) async-start(bf16[32,64,256]{2,1,0:T(8,128)(2,1)} %get-tuple-element.28), calls=%async_computation.2 | async-start | bytes 2097152 | tf_op jit(solution)/shard_map/all_to_all | solution.py:439
  223.8 33.6 %all-to-all-start.4 = ((bf16[32,64,256]{2,1,0:T(8,128)(2,1)}), bf16[32,64,256]{2,1,0:T(8,128)(2,1)S(1)}, u32[]{:S(2)}, u32[]{:S(2)}) async-start(bf16[32,64,256]{2,1,0:T(8,128)(2,1)} %finish.1), calls=%async_computation.4 | async-start | bytes 2097152 | tf_op jit(solution)/shard_map/all_to_all | solution.py:439
Sparse Core Ops, SparseCore 0:
  11.1 91.7 all-gather.2

commit v3 on v2

--- a/solution.py
+++ b/solution.py
@@ -221,7 +221,7 @@
     gathered_blocks(order, code_all, bufs, [], [e_out], block, jnp.zeros((1, 128), f32))
 
 
-def rows_kernel(places, xt_in, xt_out, xt_all, rows):
+def rows_kernel(places, xt_in, e_in, xt_out, terms_out, xt_all, rows):
     tok = xt_in.shape[2]
 
     def load(c, _):
@@ -240,20 +240,22 @@
             return 0
 
         lax.fori_loop(0, BLOCK // 128, some, 0)
-        xt_out.give(b, rows[...].reshape(BLOCK, 128).astype(bf16))
+        xt = rows[...].reshape(BLOCK, 128)
+        xt_out.give(b, xt.astype(bf16))
+        both = jnp.where(left_half((BLOCK, 128)), xt, pltpu.roll(xt, 64, 1))
+        terms_out.give(b, jnp.concatenate(split(both * e_in.take(b)), axis=1))
         return 0
 
     lax.fori_loop(0, xt_out.count, block, 0)
 
 
-def block_states(scaled, into_t):
-    p = jnp.dot(into_t, jnp.concatenate(split(scaled), axis=1), preferred_element_type=f32)
+def block_states(terms, into_t):
+    p = jnp.dot(into_t, terms, preferred_element_type=f32)
     return p[:, :128] + p[:, 128:]
 
 
-def lower_sum(scaled, from_side, into_t):
+def lower_sum(low, from_side, into_t):
     half = BLOCK // 2
-    low = scaled.astype(bf16)
     top = jnp.dot(from_side[:half], into_t[:, :half], preferred_element_type=f32)
     end = jnp.dot(from_side[half:], into_t, preferred_element_type=f32)
     keep = lower_part((half, half))
@@ -274,40 +276,35 @@
     lax.fori_loop(0, sides.count, load, 0)
 
 
-def doubled(xt):
-    x = xt.astype(f32)
-    return jnp.where(left_half((BLOCK, 128)), x, pltpu.roll(x, 64, 1))
-
-
-def states_kernel(order, write, xt_in, e_in, total, w_out, wt_out, p_out, pay_out, rows_all, *bufs):
+def states_kernel(order, write, terms_in, total, w_out, wt_out, p_out, pay_out, rows_all, *bufs):
     unpack(write, 0, rows_all)
 
     def block(b, w, summed):
         w_t = w.T.astype(bf16)
         w_out.put(b, w.astype(bf16))
         wt_out.put(b, w_t)
-        p = block_states(doubled(xt_in[b]) * e_in[b], w_t)
+        p = block_states(terms_in[b], w_t)
         p_out.put(b, p)
         return summed + p
 
     zero = jnp.zeros((128, 128), f32)
-    summed = gathered_blocks(order, rows_all, bufs, [xt_in, e_in], [w_out, wt_out, p_out], block, zero)
+    summed = gathered_blocks(order, rows_all, bufs, [terms_in], [w_out, wt_out, p_out], block, zero)
     pay = jnp.concatenate([summed, total.take(0)], axis=0)
     for g in range(pay_out.count):
         pay_out.give(g, pay)
 
 
-def near_kernel(order, read, xt_in, e_in, wt_in, q_out, qt_out, near_out, rows_all, *bufs):
+def near_kernel(order, read, terms_in, wt_in, q_out, qt_out, near_out, rows_all, *bufs):
     unpack(read, 1, rows_all)
 
     def block(b, q, _):
         q_low = q.astype(bf16)
         q_out.put(b, q_low)
         qt_out.put(b, q.T.astype(bf16))
-        near_out.put(b, lower_sum(doubled(xt_in[b]) * e_in[b], q_low, wt_in[b]))
+        near_out.put(b, lower_sum(terms_in[b][:, :128], q_low, wt_in[b]))
         return 0
 
-    gathered_blocks(order, rows_all, bufs, [xt_in, e_in, wt_in], [q_out, qt_out, near_out], block, 0)
+    gathered_blocks(order, rows_all, bufs, [terms_in, wt_in], [q_out, qt_out, near_out], block, 0)
 
 
 def prepare(unit, me, p_in, others_in, fr):
@@ -384,7 +381,7 @@
         y_out.put(b, y)
         residue = jnp.where(t < 1024.0, y.astype(f32) - t, 0.0).astype(bf16)
         res_out.put(b, residue)
-        p = block_states(residue.astype(f32) * e, from_t[b])
+        p = block_states(jnp.concatenate(split(residue.astype(f32) * e), axis=1), from_t[b])
         p_out.put(b, p)
         return summed + p
 
@@ -402,7 +399,7 @@
 
 def place_kernel(order, y_in, res_in, e_in, into_in, from_t, out, near_out, y_all, *bufs):
     def block(b):
-        near_out.put(b, lower_sum(res_in[b].astype(f32) * e_in[b], into_in[b], from_t[b]))
+        near_out.put(b, lower_sum((res_in[b].astype(f32) * e_in[b]).astype(bf16), into_in[b], from_t[b]))
         return y_in[b].astype(f32)
 
     scattered_blocks(order, bufs, y_all, [y_in, res_in, e_in, into_in, from_t], [near_out], block)
@@ -472,12 +469,15 @@
         order,
     )
     places = scan_order.reshape(length // 128, 128)
-    xt = call(rows_kernel, [by_block], [places], [head_xt], [full, small], 10**9, "rows")[0]
+    by_block_terms = struct((blocks, BLOCK, 256), bf16)
+    xt, terms = call(
+        rows_kernel, [by_block, by_block_terms], [places], [head_xt, e], [full, small], 10**9, "rows"
+    )
     w, w_t, p, pay = call(
         states_kernel,
         [by_block, by_block_t, states, payload],
         [],
-        [gathered, xt, e, total],
+        [gathered, terms, total],
         [full, small, small],
         2 * 10**9,
         "states",
@@ -488,7 +488,7 @@
         near_kernel,
         [by_block, by_block_t, wide],
         [],
-        [gathered, xt, e, w_t],
+        [gathered, terms, w_t],
         [full, small, small],
         4 * 10**9,
         "near",

time: 268 us -> 266 us (level)
  waiting for transfers between devices: 74.5 us -> 71.6 us
    all_gather x1, waiting for transfers between devices: 5.57 us -> 2.31 us  [per_device(): gathered = lax.all_gather(packet, 'space', axis=0, tiled=False)]
  transfers between devices with their start and end apart: 6 -> 6, of which waited for: 4 -> 4; matrix products, arithmetic and copies ran while one was open for 2% -> 2% of each run, Pallas kernels for 36% -> 37%
where the time goes in v3:
time: 266 us; the launch traced here: 264 us
  Pallas kernels  135 us (51%)
  waiting for transfers between devices  71.6 us (27%)
  starting transfers between devices  34.7 us (13%)
  between operations  14.8 us (6%)
  other arithmetic  4.33 us (2%)
  local copies, waits for them, and re-layouts  4.09 us (2%)
    pallas_call x8, Pallas kernels, call(): pl.pallas_call(partial(streaming, kernel, len(scalars), ordered, len(arra...  135 us
    all_to_all x5, waiting for transfers between devices, swap(): return lax.all_to_all(a, axis, split_axis=0, concat_axis=0, tiled=True)  69.3 us
    all_to_all x5, starting transfers between devices, swap(): return lax.all_to_all(a, axis, split_axis=0, concat_axis=0, tiled=True)  34.7 us
  transfers between devices with their start and end apart: 6, of which 4 were waited for; matrix products, arithmetic and copies ran while one was open for 2% of the time, Pallas kernels for 37%

profile of v3, /device:TPU:2, one launch (start us, length us, event | category | flops | bytes accessed | tf_op | source)
XLA Modules:
  0.0 264.4 jit_solution(1563047440670963455)
XLA Ops:
  7.2 1.8 packet.1
  9.1 0.7 broadcast_subtract_fusion
  9.9 1.3 broadcast_select_fusion
  11.2 1.6 pad_maximum_fusion
  12.8 11.7 %all-to-all-start = ((bf16[32,128,256]{2,1,0:T(8,128)(2,1)}), bf16[32,128,256]{2,1,0:T(8,128)(2,1)S(1)}, u32[]{:S(2)}, u32[]{:S(2)}) async-start(bf16[32,128,256]{2,1,0:T(8,128)(2,1)} %pad_maximum_fusion), calls=%async_computation | async-start | bytes 4194304 | tf_op jit(solution)/shard_map/all_to_all | solution.py:436
  25.2 21.4 %decay.1 = (f32[16,512,128]{2,1,0:T(8,128)}, f32[1,8,128]{2,1,0:T(8,128)}) custom-call(s32[16,4,128]{2,1,0:T(4,128)} %bitcast.18, f32[64,1,128]{2,1,0:T(1,128)} %convert_bitcast_fusion.refs_1_), custom_call_target="tpu_custom_call" | custom-call | flops 2000000000 | bytes 4263936 | tf_op jit(solution)/shard_map/decay/pallas_call | solution.py:25
  46.6 36.1 %all-to-all-done.refs_1_ = bf16[32,128,256]{2,1,0:T(8,128)(2,1)S(1)} async-done(((bf16[32,128,256]{2,1,0:T(8,128)(2,1)}), bf16[32,128,256]{2,1,0:T(8,128)(2,1)S(1)}, u32[]{:S(2)}, u32[]{:S(2)}) %all-to-all-start) | async-done | bytes 2097184 | tf_op jit(solution)/shard_map/all_to_all | solution.py:436
  82.8 1.3 copy-done
  84.1 16.9 %rows.1 = (bf16[16,512,128]{2,1,0:T(8,128)(2,1)}, bf16[16,512,256]{2,1,0:T(8,128)(2,1)}) custom-call(s32[64,128]{1,0:T(8,128)} %bitcast.19, bf16[32,128,256]{2,1,0:T(8,128)(2,1)} %copy-done, f32[16,512,128]{2,1,0:T(8,128)} %get-tuple-element.19.refs_2_.refs_5_.refs_3_), custom_call_target="tpu_custom_call" | custom-call | flops 1000000000 | bytes 12615680 | tf_op jit(solution)/shard_map/rows/pallas_call | solution.py:25
  101.0 2.3 all-gather.3.cloned.1.call-done
  103.3 17.7 %states.1 = (bf16[16,512,128]{2,1,0:T(8,128)(2,1)}, bf16[16,128,512]{2,1,0:T(8,128)(2,1)}, f32[16,128,128]{2,1,0:T(8,128)}, f32[8,136,128]{2,1,0:T(8,128)}) custom-call(s32[16,4,128]{2,1,0:T(4,128)} %bitcast.20, bf16[32,2,256,128]{3,2,1,0:T(8,128)(2,1)} %bitcast.15, bf16[16,512,256]{2,1,0:T(8,128)(2,1)} %get-tuple-element.20.refs_2_, ...), custom_call_target="tpu_custom_call" | custom-call | flops 2000000000 | bytes 14225408 | tf_op jit(solution)/shard_map/states/pallas_call | solution.py:25
  121.0 4.2 %all-to-all-start.1 = ((f32[8,136,128]{2,1,0:T(8,128)}), f32[8,136,128]{2,1,0:T(8,128)S(1)}, u32[]{:S(2)}, u32[]{:S(2)}) async-start(f32[8,136,128]{2,1,0:T(8,128)} %get-tuple-element.28), calls=%async_computation.1 | async-start | bytes 1114112 | tf_op jit(solution)/shard_map/all_to_all | solution.py:436
  125.8 17.5 %near.1 = (bf16[16,512,128]{2,1,0:T(8,128)(2,1)}, bf16[16,128,512]{2,1,0:T(8,128)(2,1)}, f32[16,512,128]{2,1,0:T(8,128)}) custom-call(s32[16,4,128]{2,1,0:T(4,128)} %bitcast.21, bf16[32,2,256,128]{3,2,1,0:T(8,128)(2,1)} %bitcast.16, bf16[16,512,256]{2,1,0:T(8,128)(2,1)} %get-tuple-element.20.refs_2_, bf16[16,128,512]{2,1,0:T(8,128)(2,1)} %get-tuple-element.22.refs_3_), custom_call_target="tpu_custom_call" | custom-call | flops 4000000000 | bytes 18907136 | tf_op jit(solution)/shard_map/near/pallas_call | solution.py:25
  143.3 0.8 copy-done.2
  144.1 16.2 %turn.1 = (bf16[16,512,128]{2,1,0:T(8,128)(2,1)}, bf16[16,512,128]{2,1,0:T(8,128)(2,1)}, f32[16,128,128]{2,1,0:T(8,128)}, f32[8,136,128]{2,1,0:T(8,128)}) custom-call(s32[1]{0:T(128)} %bitcast.1.refs_0_, f32[1]{0:T(128)S(6)} %copy.12.refs_1_, bf16[16,512,128]{2,1,0:T(8,128)(2,1)} %get-tuple-element.23.refs_2_, ...), custom_call_target="tpu_custom_call" | custom-call | flops 2000000000 | bytes 22089736 | tf_op jit(solution)/shard_map/turn/pallas_call | solution.py:25
  160.4 4.8 %all-to-all-start.3 = ((f32[8,136,128]{2,1,0:T(8,128)}), f32[8,136,128]{2,1,0:T(8,128)S(1)}, u32[]{:S(2)}, u32[]{:S(2)}) async-start(f32[8,136,128]{2,1,0:T(8,128)} %get-tuple-element.35), calls=%async_computation.3 | async-start | bytes 1114112 | tf_op jit(solution)/shard_map/all_to_all | solution.py:436
  165.2 21.0 %place.1 = (bf16[32,64,256]{2,1,0:T(8,128)(2,1)}, f32[16,512,128]{2,1,0:T(8,128)}) custom-call(s32[16,4,128]{2,1,0:T(4,128)} %bitcast.22, bf16[16,512,128]{2,1,0:T(8,128)(2,1)} %get-tuple-element.29.refs_1_, bf16[16,512,128]{2,1,0:T(8,128)(2,1)} %get-tuple-element.30.refs_2_.refs_4_, f32[16,512,128]{2,1,0:T(8,128)} %get-tuple-element.19.refs_2_.refs_5_.refs_3_, ...), custom_call_target="tpu_custom_call" | custom-call | flops 4000000000 | bytes 17858560 | tf_op jit(solution)/shard_map/place/pallas_call | solution.py:25
  186.2 7.7 %all-to-all-start.2 = ((bf16[32,64,256]{2,1,0:T(8,128)(2,1)}), bf16[32,64,256]{2,1,0:T(8,128)(2,1)S(1)}, u32[]{:S(2)}, u32[]{:S(2)}) async-start(bf16[32,64,256]{2,1,0:T(8,128)(2,1)} %get-tuple-element.32), calls=%async_computation.2 | async-start | bytes 2097152 | tf_op jit(solution)/shard_map/all_to_all | solution.py:436
  194.0 22.3 %finish.1 = bf16[32,64,256]{2,1,0:T(8,128)(2,1)} custom-call(s32[1]{0:T(128)} %bitcast.1.refs_0_, f32[1]{0:T(128)S(6)} %copy.12.refs_1_, s32[16,4,128]{2,1,0:T(4,128)} %bitcast.23, bf16[16,512,128]{2,1,0:T(8,128)(2,1)} %get-tuple-element.31.refs_4_.refs_3_, bf16[16,512,128]{2,1,0:T(8,128)(2,1)} %get-tuple-element.30.refs_2_.refs_4_, ...), custom_call_target="tpu_custom_call" | custom-call | flops 2000000000 | bytes 15269896 | tf_op jit(solution)/shard_map/finish/pallas_call | solution.py:25
  216.3 5.8 %all-to-all-done.2 = bf16[32,64,256]{2,1,0:T(8,128)(2,1)S(1)} async-done(((bf16[32,64,256]{2,1,0:T(8,128)(2,1)}), bf16[32,64,256]{2,1,0:T(8,128)(2,1)S(1)}, u32[]{:S(2)}, u32[]{:S(2)}) %all-to-all-start.2) | async-done | bytes 1048608 | tf_op jit(solution)/shard_map/all_to_all | solution.py:436
  222.1 6.2 %all-to-all-start.4 = ((bf16[32,64,256]{2,1,0:T(8,128)(2,1)}), bf16[32,64,256]{2,1,0:T(8,128)(2,1)S(1)}, u32[]{:S(2)}, u32[]{:S(2)}) async-start(bf16[32,64,256]{2,1,0:T(8,128)(2,1)} %finish.1), calls=%async_computation.4 | async-start | bytes 2097152 | tf_op jit(solution)/shard_map/all_to_all | solution.py:436
  228.3 27.4 %all-to-all-done.4 = bf16[32,64,256]{2,1,0:T(8,128)(2,1)S(1)} async-done(((bf16[32,64,256]{2,1,0:T(8,128)(2,1)}), bf16[32,64,256]{2,1,0:T(8,128)(2,1)S(1)}, u32[]{:S(2)}, u32[]{:S(2)}) %all-to-all-start.4) | async-done | bytes 1048608 | tf_op jit(solution)/shard_map/all_to_all | solution.py:436
  255.7 1.0 copy.13
  256.6 1.0 copy.14
  (14 shorter events, 0.8 us)
Async XLA Ops:
  7.2 4.0 %copy-start.3 = (bf16[2048,256]{1,0:T(8,128)(2,1)S(1)}, bf16[2048,256]{1,0:T(8,128)(2,1)}, u32[]{:S(2)}) copy-start(bf16[2048,256]{1,0:T(8,128)(2,1)} %param.8) | copy-start | bytes 3145732
  7.2 96.1 %all-gather.3.cloned.1.call-start = ((), (), s32[]{:S(2)}) async-start(), calls=%async_computation.5 | async-start | bytes 4325376 | tf_op jit(solution)/shard_map/all_gather | solution.py:441
  12.8 11.8 %copy-start.4 = (s32[1,8192]{1,0:T(1,128)S(1)}, s32[1,8192]{1,0:T(1,128)}, u32[]{:S(2)}) copy-start(s32[1,8192]{1,0:T(1,128)} %param.12) | copy-start | bytes 98308
  12.8 70.0 %all-to-all-start = ((bf16[32,128,256]{2,1,0:T(8,128)(2,1)}), bf16[32,128,256]{2,1,0:T(8,128)(2,1)S(1)}, u32[]{:S(2)}, u32[]{:S(2)}) async-start(bf16[32,128,256]{2,1,0:T(8,128)(2,1)} %pad_maximum_fusion), calls=%async_computation | async-start | bytes 4194304 | tf_op jit(solution)/shard_map/all_to_all | solution.py:436
  82.8 1.3 copy-start
  121.0 22.4 %all-to-all-start.1 = ((f32[8,136,128]{2,1,0:T(8,128)}), f32[8,136,128]{2,1,0:T(8,128)S(1)}, u32[]{:S(2)}, u32[]{:S(2)}) async-start(f32[8,136,128]{2,1,0:T(8,128)} %get-tuple-element.28), calls=%async_computation.1 | async-start | bytes 1114112 | tf_op jit(solution)/shard_map/all_to_all | solution.py:436
  143.3 0.8 copy-start.2
  160.4 25.8 %all-to-all-start.3 = ((f32[8,136,128]{2,1,0:T(8,128)}), f32[8,136,128]{2,1,0:T(8,128)S(1)}, u32[]{:S(2)}, u32[]{:S(2)}) async-start(f32[8,136,128]{2,1,0:T(8,128)} %get-tuple-element.35), calls=%async_computation.3 | async-start | bytes 1114112 | tf_op jit(solution)/shard_map/all_to_all | solution.py:436
  186.2 7.8 %copy-start.1 = (f32[8,136,128]{2,1,0:T(8,128)}, f32[8,136,128]{2,1,0:T(8,128)S(1)}, u32[]{:S(2)}) copy-start(f32[8,136,128]{2,1,0:T(8,128)S(1)} %all-to-all-done.3.refs_8_) | copy-start | bytes 1671172
  186.2 35.8 %all-to-all-start.2 = ((bf16[32,64,256]{2,1,0:T(8,128)(2,1)}), bf16[32,64,256]{2,1,0:T(8,128)(2,1)S(1)}, u32[]{:S(2)}, u32[]{:S(2)}) async-start(bf16[32,64,256]{2,1,0:T(8,128)(2,1)} %get-tuple-element.32), calls=%async_computation.2 | async-start | bytes 2097152 | tf_op jit(solution)/shard_map/all_to_all | solution.py:436
  222.1 33.6 %all-to-all-start.4 = ((bf16[32,64,256]{2,1,0:T(8,128)(2,1)}), bf16[32,64,256]{2,1,0:T(8,128)(2,1)S(1)}, u32[]{:S(2)}, u32[]{:S(2)}) async-start(bf16[32,64,256]{2,1,0:T(8,128)(2,1)} %finish.1), calls=%async_computation.4 | async-start | bytes 2097152 | tf_op jit(solution)/shard_map/all_to_all | solution.py:436
Sparse Core Ops, SparseCore 0:
  11.1 92.0 all-gather.2
